TPU v7x, 32 devices: a whole 2x2x4 slice. The times are simulated.
32 devices in a mesh: trow: 8 (over y, x, core), tcol: 4 (over z).
Axes of the slice: x: 2, y: 2, z: 4, core: 2. Of those that a mesh axis runs over, the one named last changes fastest.
Arguments:
- theta: float32 [25, 128, 1024], P(None, 'trow', 'tcol'), may hold values from -6 to 6
- salt: float32 [25, 128, 1024], P(None, 'trow', 'tcol'), may hold values from -6 to 6
- velocity_x: float32 [25, 128, 1024], P(None, 'trow', 'tcol'), may hold values from -0.5 to 0.5
- velocity_y: float32 [25, 128, 1024], P(None, 'trow', 'tcol'), may hold values from -0.5 to 0.5
- land_mask: int32 [25, 128, 1024], P(None, 'trow', 'tcol'), may hold values 0 or 1
- kappa: float32 [24, 128, 1024], P(None, 'trow', 'tcol'), may hold values from 0.02 to 5
- forcing: float32 [128, 1024], P('trow', 'tcol'), may hold values from -6 to 6
- bottom: int32 [128, 1024], P('trow', 'tcol'), may hold values from 0 to 25
- theta_cot: float32 [25, 128, 1024], P(None, 'trow', 'tcol'), may hold values from -6 to 6
- salt_cot: float32 [25, 128, 1024], P(None, 'trow', 'tcol'), may hold values from -6 to 6
- surface_cot: float32 [128, 1024], P('trow', 'tcol'), may hold values from -24 to 24
Outputs:
- theta_grad: float32 [25, 128, 1024], P(None, 'trow', 'tcol')
- salt_grad: float32 [25, 128, 1024], P(None, 'trow', 'tcol')
- kappa_grad: float32 [24, 128, 1024], P(None, 'trow', 'tcol')
- forcing_grad: float32 [128, 1024], P('trow', 'tcol')
All inputs are finite; a program needn't handle non-finite values. No bound on the sum of `land_mask` on one device may be relied on, other than what follows from the above.
Results may differ from a plain program's by a relative error of at most 0.0001.
Values sent between devices are 32-bit elements; how exact they have to be, the bound alone decides.
A program may use at most 64 MiB of HBM per device.

v0:
```python
import functools
import jax
import jax.numpy as jnp
from jax import lax
from jax.experimental import pallas as pl
from jax.experimental.pallas import tpu as pltpu
from jax.sharding import PartitionSpec as P

ITERS = 4


def padded_2(array, sides, width):
    for axis, dim in sides:
        peers, length = (lax.axis_size(axis), array.shape[dim])
        up = [(i, (i + 1) % peers) for i in range(peers - 1)]
        down = [(j, i) for i, j in up]
        last = lax.slice_in_dim(array, length - width, length, axis=dim)
        leading = lax.slice_in_dim(array, 0, width, axis=dim)
        before = lax.ppermute(last, axis, up)
        after = lax.ppermute(leading, axis, down)
        array = jnp.concatenate([before, array, after], axis=dim)
    return array


def cut_along(array, start, count, axis_index):
    return lax.slice_in_dim(array, start, start + count, axis=axis_index)


def join(before, array, after, axis):
    return jnp.concatenate([before, array, after], axis=axis)


def open_faces(velocity, wet, first, count, axis):
    return (
        cut_along(velocity, first, count, axis)
        * cut_along(wet, first, count, axis)
        * cut_along(wet, first + 1, count, axis)
    )


def forward_change(tracer, opened, axis, length):
    centre = cut_along(tracer, 1, length + 1, axis) + cut_along(tracer, 2, length + 1, axis)
    outer = cut_along(tracer, 0, length + 1, axis) + cut_along(tracer, 3, length + 1, axis)
    fluxes = opened * (7.0 * centre - outer) * (1.0 / 12.0)
    return cut_along(fluxes, 1, length, axis) - cut_along(fluxes, 0, length, axis)


def adjoint_change(field, opened, axis, length):
    faces = opened * (cut_along(field, 0, length + 3, axis) - cut_along(field, 1, length + 3, axis))
    return (
        7.0 * (cut_along(faces, 2, length, axis) + cut_along(faces, 1, length, axis))
        - cut_along(faces, 3, length, axis)
        - cut_along(faces, 0, length, axis)
    ) * (1.0 / 12.0)


def wet_at(land, bottom, k):
    return jnp.where(k < bottom[...], land[k].astype(jnp.float32), 0.0)


def couple_at(kappa, land, bottom, k, depth):
    below = jnp.minimum(k + 1, depth - 1)
    value = kappa[jnp.minimum(k, depth - 2)] * wet_at(land, bottom, k) * wet_at(land, bottom, below)
    return jnp.where(k < depth - 1, value, 0.0)


def rows_of(rb, ra, index, k, own):
    return join(rb[index, k], own, ra[index, k], 0)


def cols_of(rim, index, k, own):
    edge = rim[index, k]
    return join(edge[:, :2], own, edge[:, 2:], 1)


def forward_kernel(
    theta, salt, vx, vy, land, kappa, forcing, bottom, rb, ra, rim, theta_mix, salt_mix, ratios
):
    depth, rows, cols = theta.shape

    def down(k, carry):
        couple_before, ratio_before, theta_before, salt_before = carry
        wet = wet_at(land, bottom, k)
        couple = couple_at(kappa, land, bottom, k, depth)
        inverse = 1.0 / (1.0 + couple_before - couple_before * ratio_before + couple)
        ratio = couple * inverse
        ratios[k] = ratio
        open_x = open_faces(
            rows_of(rb, ra, 2, k, vx[k]), rows_of(rb, ra, 3, k, wet), 1, rows + 1, 0
        )
        open_y = open_faces(cols_of(rim, 2, k, vy[k]), cols_of(rim, 3, k, wet), 1, cols + 1, 1)
        found = []
        for index, (tracer, before) in enumerate(((theta, theta_before), (salt, salt_before))):
            own = tracer[k]
            masked = own * wet
            adv = (
                own
                - forward_change(rows_of(rb, ra, index, k, masked), open_x, 0, rows)
                - forward_change(cols_of(rim, index, k, masked), open_y, 1, cols)
            )
            if index == 0:
                adv = adv + jnp.where(k == 0, forcing[...] * wet, 0.0)
            found.append((adv + couple_before * before) * inverse)
        theta_mix[k] = found[0]
        salt_mix[k] = found[1]
        return couple, ratio, found[0], found[1]

    zero = jnp.zeros((rows, cols), jnp.float32)
    _, _, theta_last, salt_last = lax.fori_loop(0, depth, down, (zero, zero, zero, zero))

    def up(i, carry):
        k = depth - 2 - i
        a = theta_mix[k] + ratios[k] * carry[0]
        b = salt_mix[k] + ratios[k] * carry[1]
        theta_mix[k] = a
        salt_mix[k] = b
        return a, b

    lax.fori_loop(0, depth - 1, up, (theta_last, salt_last))


def mixing_kernel(
    theta_cot, salt_cot, land, kappa, bottom, zeta, theta_mix, salt_mix,
    theta_mu, salt_mu, kappa_grad, forcing_grad, ratios
):
    depth, rows, cols = theta_cot.shape

    def down(k, carry):
        couple_before, ratio_before, theta_before, salt_before = carry
        lifted = wet_at(land, bottom, k) * zeta[...]
        couple = couple_at(kappa, land, bottom, k, depth)
        inverse = 1.0 / (1.0 + couple_before - couple_before * ratio_before + couple)
        ratio = couple * inverse
        ratios[k] = ratio
        a = (theta_cot[k] + 0.2 * lifted + couple_before * theta_before) * inverse
        b = (salt_cot[k] - 0.15 * lifted + couple_before * salt_before) * inverse
        theta_mu[k] = a
        salt_mu[k] = b
        return couple, ratio, a, b

    zero = jnp.zeros((rows, cols), jnp.float32)
    _, _, theta_last, salt_last = lax.fori_loop(0, depth, down, (zero, zero, zero, zero))

    def up(i, carry):
        k = depth - 2 - i
        a = theta_mu[k] + ratios[k] * carry[0]
        b = salt_mu[k] + ratios[k] * carry[1]
        theta_mu[k] = a
        salt_mu[k] = b
        opened = wet_at(land, bottom, k) * wet_at(land, bottom, k + 1)
        kappa_grad[k] = -opened * (
            (a - carry[0]) * (theta_mix[k] - theta_mix[k + 1])
            + (b - carry[1]) * (salt_mix[k] - salt_mix[k + 1])
        )
        return a, b

    theta_top, _ = lax.fori_loop(0, depth - 1, up, (theta_last, salt_last))
    forcing_grad[...] = zeta[...] + wet_at(land, bottom, 0) * theta_top


def adjoint_kernel(
    theta_mu, salt_mu, vx, vy, land, bottom, rb, ra, rim, mu_rb, mu_ra, mu_rim, theta_grad, salt_grad
):
    depth, rows, cols = theta_mu.shape

    def level(k, carry):
        wet = wet_at(land, bottom, k)
        open_x = open_faces(
            rows_of(rb, ra, 2, k, vx[k]), rows_of(rb, ra, 3, k, wet), 0, rows + 3, 0
        )
        open_y = open_faces(cols_of(rim, 2, k, vy[k]), cols_of(rim, 3, k, wet), 0, cols + 3, 1)
        for index, (field, out) in enumerate(((theta_mu, theta_grad), (salt_mu, salt_grad))):
            own = field[k]
            out[k] = own - wet * (
                adjoint_change(rows_of(mu_rb, mu_ra, index, k, own), open_x, 0, rows)
                + adjoint_change(cols_of(mu_rim, index, k, own), open_y, 1, cols)
            )
        return carry

    lax.fori_loop(0, depth, level, 0)


LOW, HIGH = 0.2, 9.2
CENTRE, RADIUS = (HIGH + LOW) / 2, (HIGH - LOW) / 2


def times_operator(poly):
    out = [0.0] * (len(poly) + 1)
    for k, c in enumerate(poly):
        out[k] = out[k] + CENTRE * c
        if k == 0:
            out[1] = out[1] + RADIUS * c
        else:
            out[k + 1] = out[k + 1] + 0.5 * RADIUS * c
            out[k - 1] = out[k - 1] + 0.5 * RADIUS * c
    return out


def inner(p, q, moments):
    total = 0.0
    for i, a in enumerate(p):
        for j, b in enumerate(q):
            total = total + a * b * (0.5 * (moments[i + j] + moments[abs(i - j)]))
    return total


def add_scaled(p, scale, q):
    size = max(len(p), len(q))
    p = p + [0.0] * (size - len(p))
    q = q + [0.0] * (size - len(q))
    return [a + scale * b for a, b in zip(p, q)]


def weights_from(moments):
    residual = [jnp.ones_like(moments[0])]
    direction = residual
    result = []
    norm_now = moments[0]
    for iteration in range(ITERS):
        image = times_operator(direction)
        step = norm_now / inner(direction, image, moments)
        result = add_scaled(result, step, direction)
        if iteration + 1 < ITERS:
            residual = add_scaled(residual, -step, image)
            norm_next = inner(residual, residual, moments)
            direction = add_scaled(residual, norm_next / norm_now, direction)
            norm_now = norm_next
    return result


MESH = pl.DeviceIdType.MESH


def gather_kernel(lanes, piece, out, line, plane, own_sem, send, recv):
    rows, cols = lax.axis_size("trow"), lax.axis_size("tcol")
    row, col = lax.axis_index("trow"), lax.axis_index("tcol")
    peers = [(row, lax.rem(col + d, cols)) for d in range(1, cols)]
    peers += [(lax.rem(row + d, rows), col) for d in range(1, rows)]
    barrier = pltpu.get_barrier_semaphore()
    for peer in peers:
        pl.semaphore_signal(barrier, inc=1, device_id=peer, device_id_type=MESH)
    keep = pltpu.make_async_copy(piece, line.at[0], own_sem.at[0])
    keep.start()
    keep.wait()
    pl.semaphore_wait(barrier, len(peers))

    def remote(src, dst, index):
        return pltpu.make_async_remote_copy(
            src_ref=src,
            dst_ref=dst,
            send_sem=send.at[index],
            recv_sem=recv.at[index],
            device_id=peers[index],
            device_id_type=MESH,
        )

    along = [remote(piece, line.at[d], d - 1) for d in range(1, cols)]
    for copy in along:
        copy.start()
    for copy in along:
        copy.wait()
    across = [remote(line, plane.at[d - 1], cols + d - 2) for d in range(1, rows)]
    for copy in across:
        copy.start()
    total = line[0]
    for d in range(1, cols):
        total = total + line[d]
    for copy in across:
        copy.wait()
    for d in range(rows - 1):
        for e in range(cols):
            total = total + plane[d, e]
    out[...] = total


def sum_everywhere(sums):
    rows, cols = lax.axis_size("trow"), lax.axis_size("tcol")
    lanes = 128
    piece = jnp.broadcast_to(jnp.pad(sums, (0, lanes - sums.shape[0]))[None], (8, lanes))
    count = rows + cols - 2
    total = pl.pallas_call(
        functools.partial(gather_kernel, lanes),
        out_shape=jax.ShapeDtypeStruct((8, lanes), jnp.float32),
        in_specs=[pl.BlockSpec(memory_space=pltpu.VMEM)],
        out_specs=pl.BlockSpec(memory_space=pltpu.VMEM),
        scratch_shapes=[
            pltpu.VMEM((cols, 8, lanes), jnp.float32),
            pltpu.VMEM((rows - 1, cols, 8, lanes), jnp.float32),
            pltpu.SemaphoreType.DMA((1,)),
            pltpu.SemaphoreType.DMA((count,)),
            pltpu.SemaphoreType.DMA((count,)),
        ],
        compiler_params=pltpu.CompilerParams(collective_id=0, has_side_effects=True),
    )(piece)
    return total[0, : sums.shape[0]]


def conjugate(target, bottom, depth):
    rows, cols = target.shape
    rim = ITERS
    padded = padded_2(jnp.stack([target, bottom.astype(jnp.float32)]), (("trow", 1), ("tcol", 2)), rim)
    row = lax.broadcasted_iota(jnp.int32, (rows + 2 * rim, 1), 0) - rim + lax.axis_index("trow") * rows
    col = lax.broadcasted_iota(jnp.int32, (1, cols + 2 * rim), 1) - rim + lax.axis_index("tcol") * cols
    inside = ((row >= 0) & (row < rows * lax.axis_size("trow"))) & (
        (col >= 0) & (col < cols * lax.axis_size("tcol"))
    )
    scaled = (4.2 - CENTRE + padded[1] / depth) / RADIUS
    basis = [padded[0]]
    for k in range(ITERS):
        field = basis[-1]
        edge = k + 1
        beside = field[2:, 1:-1] + field[:-2, 1:-1] + field[1:-1, 2:] + field[1:-1, :-2]
        image = scaled[edge:-edge, edge:-edge] * field[1:-1, 1:-1] - beside * (1.0 / RADIUS)
        if k > 0:
            image = 2.0 * image - basis[-2][2:-2, 2:-2]
        basis.append(jnp.where(inside[edge:-edge, edge:-edge], image, 0.0))
    own = [f[rim - k : rim - k + rows, rim - k : rim - k + cols] for k, f in enumerate(basis)]
    sums = [jnp.sum(own[0] * own[k]) for k in range(5)]
    sums += [jnp.sum(own[2] * own[3]), jnp.sum(own[3] * own[3]), jnp.sum(own[3] * own[4])]
    m = list(sum_everywhere(jnp.stack(sums)))
    m = m[:5] + [2.0 * m[5] - m[1], 2.0 * m[6] - m[0], 2.0 * m[7] - m[1]]
    weights = weights_from(m)
    result = weights[0] * own[0]
    for k in range(1, ITERS):
        result = result + weights[k] * own[k]
    return result


def call(kernel, outs, scratch, args):
    size = sum(a.size for a in args) * 4
    return pl.pallas_call(
        kernel,
        out_shape=[jax.ShapeDtypeStruct(o, jnp.float32) for o in outs],
        in_specs=[pl.BlockSpec(memory_space=pltpu.VMEM)] * len(args),
        out_specs=[pl.BlockSpec(memory_space=pltpu.VMEM)] * len(outs),
        scratch_shapes=[pltpu.VMEM(o, jnp.float32) for o in scratch],
        compiler_params=pltpu.CompilerParams(vmem_limit_bytes=40 * 1024 * 1024),
        cost_estimate=pl.CostEstimate(flops=size * 20, bytes_accessed=size, transcendentals=0),
    )(*args)


def from_neighbours(first, last, axis):
    peers = lax.axis_size(axis)
    up = [(i, (i + 1) % peers) for i in range(peers - 1)]
    down = [(j, i) for i, j in up]
    return lax.ppermute(last, axis, up), lax.ppermute(first, axis, down)


def row_rims(fields):
    return from_neighbours(
        jnp.stack([f[:, :2] for f in fields]), jnp.stack([f[:, -2:] for f in fields]), "trow"
    )


def col_rims(fields):
    before, after = from_neighbours(
        jnp.stack([f[:, :, :2].swapaxes(1, 2) for f in fields]),
        jnp.stack([f[:, :, -2:].swapaxes(1, 2) for f in fields]),
        "tcol",
    )
    return jnp.concatenate([before, after], axis=2).swapaxes(2, 3)


def shards(
    theta,
    salt,
    velocity_x,
    velocity_y,
    land_mask,
    kappa,
    forcing,
    bottom,
    theta_cot,
    salt_cot,
    surface_cot,
):
    depth, rows, cols = theta.shape
    levels = lax.broadcasted_iota(jnp.int32, (depth, 1, 1), 0)
    wet = land_mask.astype(jnp.float32) * (levels < bottom[None]).astype(jnp.float32)
    rb, ra = row_rims([theta * wet, salt * wet, velocity_x, wet])
    rim = col_rims([theta * wet, salt * wet, velocity_y, wet])
    whole = (depth, rows, cols)
    theta_mix, salt_mix = call(
        forward_kernel,
        [whole, whole],
        [whole],
        (theta, salt, velocity_x, velocity_y, land_mask, kappa, forcing, bottom, rb, ra, rim),
    )
    zeta = conjugate(surface_cot, bottom, depth)
    theta_mu, salt_mu, kappa_grad, forcing_grad = call(
        mixing_kernel,
        [whole, whole, (depth - 1, rows, cols), (rows, cols)],
        [whole],
        (theta_cot, salt_cot, land_mask, kappa, bottom, zeta, theta_mix, salt_mix),
    )
    mu_rb, mu_ra = row_rims([theta_mu, salt_mu])
    mu_rim = col_rims([theta_mu, salt_mu])
    theta_grad, salt_grad = call(
        adjoint_kernel,
        [whole, whole],
        [],
        (theta_mu, salt_mu, velocity_x, velocity_y, land_mask, bottom, rb, ra, rim, mu_rb, mu_ra, mu_rim),
    )
    return (theta_grad, salt_grad, kappa_grad, forcing_grad)


def solution(mesh):
    in_specs = (
        P(None, "trow", "tcol"),
        P(None, "trow", "tcol"),
        P(None, "trow", "tcol"),
        P(None, "trow", "tcol"),
        P(None, "trow", "tcol"),
        P(None, "trow", "tcol"),
        P("trow", "tcol"),
        P("trow", "tcol"),
        P(None, "trow", "tcol"),
        P(None, "trow", "tcol"),
        P("trow", "tcol"),
    )
    out_specs = (
        P(None, "trow", "tcol"),
        P(None, "trow", "tcol"),
        P(None, "trow", "tcol"),
        P("trow", "tcol"),
    )
    return jax.shard_map(shards, mesh=mesh, in_specs=in_specs, out_specs=out_specs, check_vma=False)
```

profile of v0, /device:TPU:1, one launch (start us, length us, event | category | flops | bytes accessed | tf_op | source)
XLA Modules:
  0.0 127.3 jit_solution(1504643972608212589)
XLA Ops:
  0.6 0.7 convert_bitcast_fusion
  1.4 0.6 pad_maximum_fusion.13
  2.0 4.5 %collective-permute-start = (f32[2,4,256]{2,1,0:T(4,128)}, f32[2,4,256]{2,1,0:T(4,128)S(1)}, u32[]{:S(2)}, u32[]{:S(2)}) collective-permute-start(f32[2,4,256]{2,1,0:T(4,128)} %get-tuple-element.58), channel_id=1, source_target_pairs={{0,4},{4,8},{8,12},{12,16},{16,20},{20,24},{24,28},{1,5},{5,9},{9,... | collective-permute-start | bytes 24584 | tf_op jit(solution)/shard_map/ppermute | solution.py:19
  6.5 2.1 %collective-permute-start.1 = (f32[2,4,256]{2,1,0:T(4,128)}, f32[2,4,256]{2,1,0:T(4,128)}, u32[]{:S(2)}, u32[]{:S(2)}) collective-permute-start(f32[2,4,256]{2,1,0:T(4,128)} %get-tuple-element.59), channel_id=1, source_target_pairs={{4,0},{8,4},{12,8},{16,12},{20,16},{24,20},{28,24},{5,1},{9,5},{13... | collective-permute-start | bytes 24584 | tf_op jit(solution)/shard_map/ppermute | solution.py:20
  8.6 1.1 fusion.23
  9.7 0.2 copy.30
  9.9 0.5 copy-done.6
  10.4 0.1 fusion.22
  10.5 0.9 copy-done.4
  11.5 0.2 slice_bitcast_fusion.3
  11.7 0.8 copy.22
  12.5 0.8 copy.20
  13.3 0.1 slice_bitcast_fusion.4
  13.4 0.8 copy.21
  14.2 1.4 %pad_maximum_fusion.7 = f32[4,25,2,16]{1,3,2,0:T(8,128)} fusion(f32[1,25,2,16]{1,3,2,0:T(8,128)} %copy.22, f32[1,25,2,16]{1,3,2,0:T(8,128)S(1)} %bitcast.101, f32[1,25,2,16]{1,3,2,0:T(8,128)} %copy.21, f32[1,25,2,16]{1,3,2,0:T(8,128)} %copy.20), kind=kLoop, calls=%fused_computation.19 | loop fusion | flops 9600 | bytes 25600 | tf_op jit(solution)/shard_map/stack | solution.py:357
  15.6 1.3 %collective-permute-start.7 = (f32[4,25,2,16]{1,3,2,0:T(8,128)}, f32[4,25,2,16]{1,3,2,0:T(8,128)}, u32[]{:S(2)}, u32[]{:S(2)}) collective-permute-start(f32[4,25,2,16]{1,3,2,0:T(8,128)} %pad_maximum_fusion.7), channel_id=1, source_target_pairs={{1,0},{2,1},{3,2},{5,4},{6,5},{7,6},{9,8},{10,9},{11,10},{13,12},{... | collective-permute-start | bytes 38408 | tf_op jit(solution)/shard_map/ppermute | solution.py:346
  16.9 0.2 copy.29
  17.1 0.8 copy.18
  17.9 0.2 copy.16
  18.1 0.2 copy.17
  18.3 0.3 copy-done.15
  18.6 0.6 pad_maximum_fusion.6
  19.2 4.6 %collective-permute-start.6 = (f32[4,25,2,16]{1,3,2,0:T(8,128)}, f32[4,25,2,16]{1,3,2,0:T(8,128)}, u32[]{:S(2)}, u32[]{:S(2)}) collective-permute-start(f32[4,25,2,16]{1,3,2,0:T(8,128)} %pad_maximum_fusion.6), channel_id=1, source_target_pairs={{0,1},{1,2},{2,3},{4,5},{5,6},{6,7},{8,9},{9,10},{10,11},{12,13},{... | collective-permute-start | bytes 38408 | tf_op jit(solution)/shard_map/ppermute | solution.py:346
  24.0 0.8 pad_maximum_fusion
  24.8 4.2 %collective-permute-start.4 = (f32[4,25,2,256]{3,2,1,0:T(2,128)}, f32[4,25,2,256]{3,2,1,0:T(2,128)S(1)}, u32[]{:S(2)}, u32[]{:S(2)}) collective-permute-start(f32[4,25,2,256]{3,2,1,0:T(2,128)} %pad_maximum_fusion), channel_id=1, source_target_pairs={{0,4},{4,8},{8,12},{12,16},{16,20},{20,24},{24,28},{1,5},{5,9},{9,... | collective-permute-start | bytes 614408 | tf_op jit(solution)/shard_map/ppermute | solution.py:346
  29.0 0.1 broadcast_and_fusion
  29.1 0.7 pad_maximum_fusion.9
  29.9 2.6 %collective-permute-start.2 = (f32[2,24,4]{2,1,0:T(8,128)S(1)}, f32[2,24,4]{2,1,0:T(8,128)S(1)}, u32[]{:S(2)}, u32[]{:S(2)}) collective-permute-start(f32[2,24,4]{2,1,0:T(8,128)S(1)} %get-tuple-element.56), channel_id=1, source_target_pairs={{0,1},{1,2},{2,3},{4,5},{5,6},{6,7},{8,9},{9,10},{10,11},{12,13},{... | collective-permute-start | bytes 2312 | tf_op jit(solution)/shard_map/ppermute | solution.py:19
  32.5 1.3 %collective-permute-start.3 = (f32[2,24,4]{2,1,0:T(8,128)S(1)}, f32[2,24,4]{2,1,0:T(8,128)S(1)}, u32[]{:S(2)}, u32[]{:S(2)}) collective-permute-start(f32[2,24,4]{2,1,0:T(8,128)S(1)} %get-tuple-element.57), channel_id=1, source_target_pairs={{1,0},{2,1},{3,2},{5,4},{6,5},{7,6},{9,8},{10,9},{11,10},{13,12},{... | collective-permute-start | bytes 2312 | tf_op jit(solution)/shard_map/ppermute | solution.py:20
  33.8 0.8 pad_maximum_fusion.1
  34.6 1.9 %collective-permute-start.5 = (f32[4,25,2,256]{3,2,1,0:T(2,128)}, f32[4,25,2,256]{3,2,1,0:T(2,128)}, u32[]{:S(2)}, u32[]{:S(2)}) collective-permute-start(f32[4,25,2,256]{3,2,1,0:T(2,128)} %pad_maximum_fusion.1), channel_id=1, source_target_pairs={{4,0},{8,4},{12,8},{16,12},{20,16},{24,20},{28,24},{5,1},{9,5},{13... | collective-permute-start | bytes 614408 | tf_op jit(solution)/shard_map/ppermute | solution.py:346
  36.5 1.0 collective-permute-done.3
  37.5 0.8 pad_maximum_fusion.5
  38.3 0.1 fusion.10
  38.5 0.1 fusion.4
  38.6 0.1 fusion
  38.8 0.8 multiply_reduce_fusion
  39.6 5.0 %stack.143 = f32[8]{0:T(128)S(1)} concatenate(f32[1]{0:T(128)} %bitcast.3, f32[1]{0:T(128)} %bitcast.5, f32[1]{0:T(128)} %bitcast.6, f32[1]{0:T(128)} %bitcast.7, f32[1]{0:T(128)} %bitcast.8, f32[1]{0:T(128)} %bitcast.9, f32[1]{0:T(128)} %bitcast.10, f32[1]{0:T(128)} %bitcast.11), dimensions={0} | concatenate | bytes 64 | tf_op jit(solution)/shard_map/stack | solution.py:320
  44.5 0.6 broadcast_in_dim.27.piece
  45.1 13.1 %shard_map.138 = f32[8,128]{1,0:T(8,128)} custom-call(f32[8,128]{1,0:T(8,128)} %broadcast_in_dim.27.piece), custom_call_target="tpu_custom_call" | custom-call | tf_op jit(solution)/shard_map/pallas_call | solution.py:281
  58.3 1.6 %fusion.25 = (f32[1,1]{1,0:T(1,128)}, f32[1,1]{1,0:T(1,128)}, f32[1,1]{1,0:T(1,128)}, f32[1,1]{1,0:T(1,128)}, f32[1,1]{1,0:T(1,128)}, /*index=5*/f32[1,1]{1,0:T(1,128)}, f32[1,1]{1,0:T(1,128)}, f32[1,1]{1,0:T(1,128)}) fusion(f32[8,128]{1,0:T(8,128)} %shard_map.138), kind=kLoop, calls=%fused_computation.96 | loop fusion | bytes 64 | tf_op jit(solution)/shard_map/unstack | solution.py:320
  79.6 0.1 multiply_add_fusion.zeta
  79.7 1.5 %pad_maximum_fusion.2 = f32[4,25,4,16]{1,3,2,0:T(8,128)} fusion(f32[4,25,2,16]{1,3,2,0:T(8,128)} %collective-permute-done.7, f32[4,25,2,16]{1,3,2,0:T(8,128)} %collective-permute-done.6), kind=kLoop, calls=%fused_computation.14 | loop fusion | flops 6400 | bytes 51200 | tf_op jit(solution)/shard_map/concatenate | solution.py:361
  81.3 1.5 %copy.23 = f32[4,25,4,16]{2,3,1,0:T(8,128)S(1)} copy(f32[4,25,4,16]{1,3,2,0:T(8,128)} %pad_maximum_fusion.2) | data formatting | bytes 51200 | tf_op jit(solution)/shard_map/concatenate | solution.py:361
  82.9 10.7 %shard_map.139 = (f32[25,16,256]{2,1,0:T(8,128)S(1)}, f32[25,16,256]{2,1,0:T(8,128)S(1)}) custom-call(f32[25,16,256]{2,1,0:T(8,128)S(1)} %copy-done.3, f32[25,16,256]{2,1,0:T(8,128)S(1)} %copy-done.4, f32[25,16,256]{2,1,0:T(8,128)S(1)} %copy-done.2, f32[25,16,256]{2,1,0:T(8,128)S(1)} %copy-done.1, s32[25,16,256]{2,1,0:T(8,128)S(1)} %copy-done, ...), custom_call_target="tpu_custom_call" | custom-call | flops 58183680 | bytes 2909184 | tf_op jit(solution)/shard_map/pallas_call | solution.py:331
  93.6 1.6 %shard_map.140 = (f32[25,16,256]{2,1,0:T(8,128)S(1)}, f32[25,16,256]{2,1,0:T(8,128)S(1)}, f32[24,16,256]{2,1,0:T(8,128)}, f32[16,256]{1,0:T(8,128)}) custom-call(f32[25,16,256]{2,1,0:T(8,128)S(1)} %copy-done.7, f32[25,16,256]{2,1,0:T(8,128)S(1)} %copy-done.8, s32[25,16,256]{2,1,0:T(8,128)S(1)} %copy-done, f32[24,16,256]{2,1,0:T(8,128)S(1)} %copy-done.5, ...), custom_call_target="tpu_custom_call" | custom-call | flops 49479680 | bytes 2473984 | tf_op jit(solution)/shard_map/pallas_call | solution.py:331
  95.2 0.1 slice_bitcast_fusion.9
  95.4 0.7 slice_bitcast_fusion.16
  96.0 0.8 slice_bitcast_fusion.8
  96.8 0.7 pad_maximum_fusion.3
  97.5 3.4 %collective-permute-start.8 = (f32[2,25,2,256]{3,2,1,0:T(2,128)}, f32[2,25,2,256]{3,2,1,0:T(2,128)}, u32[]{:S(2)}, u32[]{:S(2)}) collective-permute-start(f32[2,25,2,256]{3,2,1,0:T(2,128)} %pad_maximum_fusion.3), channel_id=1, source_target_pairs={{0,4},{4,8},{8,12},{12,16},{16,20},{20,24},{24,28},{1,5},{5,9},{9,... | collective-permute-start | bytes 307208 | tf_op jit(solution)/shard_map/ppermute | solution.py:346
  100.9 0.8 copy.24
  101.7 0.8 copy.26
  102.5 1.1 copy.25
  103.6 0.2 copy.27
  103.8 0.5 copy-done.14
  104.3 1.4 %collective-permute-start.11 = (f32[2,25,2,16]{1,3,2,0:T(8,128)S(1)}, f32[2,25,2,16]{1,3,2,0:T(8,128)S(1)}, u32[]{:S(2)}, u32[]{:S(2)}) collective-permute-start(f32[2,25,2,16]{1,3,2,0:T(8,128)S(1)} %pad_maximum_fusion.11), channel_id=1, source_target_pairs={{1,0},{2,1},{3,2},{5,4},{6,5},{7,6},{9,8},{10,9},{11,10},{13,12},{... | collective-permute-start | bytes 19208 | tf_op jit(solution)/shard_map/ppermute | solution.py:346
  105.8 4.0 %collective-permute-start.10 = (f32[2,25,2,16]{1,3,2,0:T(8,128)S(1)}, f32[2,25,2,16]{1,3,2,0:T(8,128)S(1)}, u32[]{:S(2)}, u32[]{:S(2)}) collective-permute-start(f32[2,25,2,16]{1,3,2,0:T(8,128)S(1)} %pad_maximum_fusion.10), channel_id=1, source_target_pairs={{0,1},{1,2},{2,3},{4,5},{5,6},{6,7},{8,9},{9,10},{10,11},{12,13},{... | collective-permute-start | bytes 19208 | tf_op jit(solution)/shard_map/ppermute | solution.py:346
  109.8 0.7 pad_maximum_fusion.4
  110.5 2.1 %collective-permute-start.9 = (f32[2,25,2,256]{3,2,1,0:T(2,128)}, f32[2,25,2,256]{3,2,1,0:T(2,128)}, u32[]{:S(2)}, u32[]{:S(2)}) collective-permute-start(f32[2,25,2,256]{3,2,1,0:T(2,128)} %pad_maximum_fusion.4), channel_id=1, source_target_pairs={{4,0},{8,4},{12,8},{16,12},{20,16},{24,20},{28,24},{5,1},{9,5},{13... | collective-permute-start | bytes 307208 | tf_op jit(solution)/shard_map/ppermute | solution.py:346
  112.7 0.6 pad_maximum_fusion.8
  113.3 1.2 copy.28
  114.5 2.3 %collective-permute-done.9.mu_ra = f32[2,25,2,256]{3,2,1,0:T(2,128)} collective-permute-done((f32[2,25,2,256]{3,2,1,0:T(2,128)}, f32[2,25,2,256]{3,2,1,0:T(2,128)}, u32[]{:S(2)}, u32[]{:S(2)}) %collective-permute-start.9) | collective-permute-done | bytes 102432 | tf_op jit(solution)/shard_map/ppermute | solution.py:346
  116.8 10.6 %shard_map.141 = (f32[25,16,256]{2,1,0:T(8,128)}, f32[25,16,256]{2,1,0:T(8,128)}) custom-call(f32[25,16,256]{2,1,0:T(8,128)S(1)} %get-tuple-element.14.theta_mu, f32[25,16,256]{2,1,0:T(8,128)S(1)} %get-tuple-element.15.salt_mu, f32[25,16,256]{2,1,0:T(8,128)S(1)} %copy-done.2, f32[25,16,256]{2,1,0:T(8,128)S(1)} %copy-done.1, s32[25,16,256]{2,1,0:T(8,128)S(1)} %copy-done, ...), custom_call_target="tpu_custom_call" | custom-call | flops 54343680 | bytes 2717184 | tf_op jit(solution)/shard_map/pallas_call | solution.py:331
  (49 shorter events, 0.5 us)
Async XLA Ops:
  0.6 0.7 copy-start.12
  2.0 27.1 %collective-permute-start = (f32[2,4,256]{2,1,0:T(4,128)}, f32[2,4,256]{2,1,0:T(4,128)S(1)}, u32[]{:S(2)}, u32[]{:S(2)}) collective-permute-start(f32[2,4,256]{2,1,0:T(4,128)} %get-tuple-element.58), channel_id=1, source_target_pairs={{0,4},{4,8},{8,12},{12,16},{16,20},{20,24},{24,28},{1,5},{5,9},{9,... | collective-permute-start | bytes 24584 | tf_op jit(solution)/shard_map/ppermute | solution.py:19
  6.5 3.5 %copy-start = (s32[25,16,256]{2,1,0:T(8,128)S(1)}, s32[25,16,256]{2,1,0:T(8,128)}, u32[]{:S(2)}) copy-start(s32[25,16,256]{2,1,0:T(8,128)} %land.5) | copy-start | bytes 1228804
  6.5 3.4 %copy-start.3 = (f32[25,16,256]{2,1,0:T(8,128)S(1)}, f32[25,16,256]{2,1,0:T(8,128)}, u32[]{:S(2)}) copy-start(f32[25,16,256]{2,1,0:T(8,128)} %theta.1) | copy-start | bytes 1228804
  6.5 22.6 %collective-permute-start.1 = (f32[2,4,256]{2,1,0:T(4,128)}, f32[2,4,256]{2,1,0:T(4,128)}, u32[]{:S(2)}, u32[]{:S(2)}) collective-permute-start(f32[2,4,256]{2,1,0:T(4,128)} %get-tuple-element.59), channel_id=1, source_target_pairs={{4,0},{8,4},{12,8},{16,12},{20,16},{24,20},{28,24},{5,1},{9,5},{13... | collective-permute-start | bytes 24584 | tf_op jit(solution)/shard_map/ppermute | solution.py:20
  9.7 0.7 copy-start.6
  10.4 1.0 copy-start.4
  15.6 64.1 %collective-permute-start.7 = (f32[4,25,2,16]{1,3,2,0:T(8,128)}, f32[4,25,2,16]{1,3,2,0:T(8,128)}, u32[]{:S(2)}, u32[]{:S(2)}) collective-permute-start(f32[4,25,2,16]{1,3,2,0:T(8,128)} %pad_maximum_fusion.7), channel_id=1, source_target_pairs={{1,0},{2,1},{3,2},{5,4},{6,5},{7,6},{9,8},{10,9},{11,10},{13,12},{... | collective-permute-start | bytes 38408 | tf_op jit(solution)/shard_map/ppermute | solution.py:346
  17.9 0.7 copy-start.15
  18.1 5.8 %copy-start.2 = (f32[25,16,256]{2,1,0:T(8,128)S(1)}, f32[25,16,256]{2,1,0:T(8,128)}, u32[]{:S(2)}) copy-start(f32[25,16,256]{2,1,0:T(8,128)} %vx.3) | copy-start | bytes 1228804
  19.2 60.5 %collective-permute-start.6 = (f32[4,25,2,16]{1,3,2,0:T(8,128)}, f32[4,25,2,16]{1,3,2,0:T(8,128)}, u32[]{:S(2)}, u32[]{:S(2)}) collective-permute-start(f32[4,25,2,16]{1,3,2,0:T(8,128)} %pad_maximum_fusion.6), channel_id=1, source_target_pairs={{0,1},{1,2},{2,3},{4,5},{5,6},{6,7},{8,9},{9,10},{10,11},{12,13},{... | collective-permute-start | bytes 38408 | tf_op jit(solution)/shard_map/ppermute | solution.py:346
  24.8 58.0 %collective-permute-start.4 = (f32[4,25,2,256]{3,2,1,0:T(2,128)}, f32[4,25,2,256]{3,2,1,0:T(2,128)S(1)}, u32[]{:S(2)}, u32[]{:S(2)}) collective-permute-start(f32[4,25,2,256]{3,2,1,0:T(2,128)} %pad_maximum_fusion), channel_id=1, source_target_pairs={{0,4},{4,8},{8,12},{12,16},{16,20},{20,24},{24,28},{1,5},{5,9},{9,... | collective-permute-start | bytes 614408 | tf_op jit(solution)/shard_map/ppermute | solution.py:346
  29.9 4.7 %collective-permute-start.2 = (f32[2,24,4]{2,1,0:T(8,128)S(1)}, f32[2,24,4]{2,1,0:T(8,128)S(1)}, u32[]{:S(2)}, u32[]{:S(2)}) collective-permute-start(f32[2,24,4]{2,1,0:T(8,128)S(1)} %get-tuple-element.56), channel_id=1, source_target_pairs={{0,1},{1,2},{2,3},{4,5},{5,6},{6,7},{8,9},{9,10},{10,11},{12,13},{... | collective-permute-start | bytes 2312 | tf_op jit(solution)/shard_map/ppermute | solution.py:19
  32.5 5.0 %collective-permute-start.3 = (f32[2,24,4]{2,1,0:T(8,128)S(1)}, f32[2,24,4]{2,1,0:T(8,128)S(1)}, u32[]{:S(2)}, u32[]{:S(2)}) collective-permute-start(f32[2,24,4]{2,1,0:T(8,128)S(1)} %get-tuple-element.57), channel_id=1, source_target_pairs={{1,0},{2,1},{3,2},{5,4},{6,5},{7,6},{9,8},{10,9},{11,10},{13,12},{... | collective-permute-start | bytes 2312 | tf_op jit(solution)/shard_map/ppermute | solution.py:20
  34.6 48.2 %collective-permute-start.5 = (f32[4,25,2,256]{3,2,1,0:T(2,128)}, f32[4,25,2,256]{3,2,1,0:T(2,128)}, u32[]{:S(2)}, u32[]{:S(2)}) collective-permute-start(f32[4,25,2,256]{3,2,1,0:T(2,128)} %pad_maximum_fusion.1), channel_id=1, source_target_pairs={{4,0},{8,4},{12,8},{16,12},{20,16},{24,20},{28,24},{5,1},{9,5},{13... | collective-permute-start | bytes 614408 | tf_op jit(solution)/shard_map/ppermute | solution.py:346
  81.3 1.5 %copy-start.1 = (f32[25,16,256]{2,1,0:T(8,128)S(1)}, f32[25,16,256]{2,1,0:T(8,128)}, u32[]{:S(2)}) copy-start(f32[25,16,256]{2,1,0:T(8,128)} %vy.3) | copy-start | bytes 1228804
  81.3 1.5 %copy-start.5 = (f32[24,16,256]{2,1,0:T(8,128)S(1)}, f32[24,16,256]{2,1,0:T(8,128)}, u32[]{:S(2)}) copy-start(f32[24,16,256]{2,1,0:T(8,128)} %kappa.3) | copy-start | bytes 1179652
  81.3 1.5 %copy-start.9 = (f32[16,256]{1,0:T(8,128)S(1)}, f32[16,256]{1,0:T(8,128)}, u32[]{:S(2)}) copy-start(f32[16,256]{1,0:T(8,128)} %forcing.1) | copy-start | bytes 49156
  82.8 10.7 %copy-start.7 = (f32[25,16,256]{2,1,0:T(8,128)S(1)}, f32[25,16,256]{2,1,0:T(8,128)}, u32[]{:S(2)}) copy-start(f32[25,16,256]{2,1,0:T(8,128)} %theta_cot.1) | copy-start | bytes 1228804
  82.8 10.7 %copy-start.8 = (f32[25,16,256]{2,1,0:T(8,128)S(1)}, f32[25,16,256]{2,1,0:T(8,128)}, u32[]{:S(2)}) copy-start(f32[25,16,256]{2,1,0:T(8,128)} %salt_cot.1) | copy-start | bytes 1228804
  97.5 16.9 %collective-permute-start.8 = (f32[2,25,2,256]{3,2,1,0:T(2,128)}, f32[2,25,2,256]{3,2,1,0:T(2,128)}, u32[]{:S(2)}, u32[]{:S(2)}) collective-permute-start(f32[2,25,2,256]{3,2,1,0:T(2,128)} %pad_maximum_fusion.3), channel_id=1, source_target_pairs={{0,4},{4,8},{8,12},{12,16},{16,20},{20,24},{24,28},{1,5},{5,9},{9,... | collective-permute-start | bytes 307208 | tf_op jit(solution)/shard_map/ppermute | solution.py:346
  101.7 1.9 %copy-start.10 = (f32[1,25,2,16]{2,3,1,0:T(8,128)S(1)}, f32[1,25,2,16]{2,3,1,0:T(8,128)}, u32[]{:S(2)}) copy-start(f32[1,25,2,16]{2,3,1,0:T(8,128)} %get-tuple-element.33) | copy-start | bytes 9604
  103.6 0.7 copy-start.14
  103.6 2.2 %copy-start.13 = (f32[1,25,2,16]{1,3,2,0:T(8,128)S(1)}, f32[1,25,2,16]{1,3,2,0:T(8,128)}, u32[]{:S(2)}) copy-start(f32[1,25,2,16]{1,3,2,0:T(8,128)} %copy.24) | copy-start | bytes 9604
  104.3 5.5 %copy-start.11 = (f32[1,25,2,256]{3,2,1,0:T(2,128)S(1)}, f32[1,25,2,256]{3,2,1,0:T(2,128)}, u32[]{:S(2)}) copy-start(f32[1,25,2,256]{3,2,1,0:T(2,128)} %get-tuple-element.36) | copy-start | bytes 153604
  104.3 8.3 %collective-permute-start.11 = (f32[2,25,2,16]{1,3,2,0:T(8,128)S(1)}, f32[2,25,2,16]{1,3,2,0:T(8,128)S(1)}, u32[]{:S(2)}, u32[]{:S(2)}) collective-permute-start(f32[2,25,2,16]{1,3,2,0:T(8,128)S(1)} %pad_maximum_fusion.11), channel_id=1, source_target_pairs={{1,0},{2,1},{3,2},{5,4},{6,5},{7,6},{9,8},{10,9},{11,10},{13,12},{... | collective-permute-start | bytes 19208 | tf_op jit(solution)/shard_map/ppermute | solution.py:346
  105.8 6.9 %collective-permute-start.10 = (f32[2,25,2,16]{1,3,2,0:T(8,128)S(1)}, f32[2,25,2,16]{1,3,2,0:T(8,128)S(1)}, u32[]{:S(2)}, u32[]{:S(2)}) collective-permute-start(f32[2,25,2,16]{1,3,2,0:T(8,128)S(1)} %pad_maximum_fusion.10), channel_id=1, source_target_pairs={{0,1},{1,2},{2,3},{4,5},{5,6},{6,7},{8,9},{9,10},{10,11},{12,13},{... | collective-permute-start | bytes 19208 | tf_op jit(solution)/shard_map/ppermute | solution.py:346
  110.5 6.3 %collective-permute-start.9 = (f32[2,25,2,256]{3,2,1,0:T(2,128)}, f32[2,25,2,256]{3,2,1,0:T(2,128)}, u32[]{:S(2)}, u32[]{:S(2)}) collective-permute-start(f32[2,25,2,256]{3,2,1,0:T(2,128)} %pad_maximum_fusion.4), channel_id=1, source_target_pairs={{4,0},{8,4},{12,8},{16,12},{20,16},{24,20},{28,24},{5,1},{9,5},{13... | collective-permute-start | bytes 307208 | tf_op jit(solution)/shard_map/ppermute | solution.py:346
where the time goes:
time: 129 us; the launch traced here: 127 us
  Pallas kernels  36 us (28%)
  starting transfers between devices  33.3 us (26%)
  local copies, waits for them, and re-layouts  22.4 us (17%)
  between operations  20.8 us (16%)
  other arithmetic  11.5 us (9%)
  waiting for transfers between devices  3.37 us (3%)
    ppermute x8, starting transfers between devices, from_neighbours(): return (lax.ppermute(last, axis, up), lax.ppermute(first, axis, down))  22.9 us
    pallas_call x3, Pallas kernels, call(): pl.pallas_call(kernel, out_shape=[jax.ShapeDtypeStruct(o, jnp.float32) fo...  22.9 us
    pallas_call x1, Pallas kernels, sum_everywhere(): pl.pallas_call(functools.partial(gather_kernel, lanes), out_shape=jax.Sha...  13.1 us
    ppermute x2, starting transfers between devices, padded_2(): before = lax.ppermute(last, axis, up)  7.07 us
    another operation x2, local copies, waits for them, and re-layouts, conjugate(): m = list(sum_everywhere(jnp.stack(sums)))  6.6 us
    another operation x9, local copies, waits for them, and re-layouts, col_rims(): jnp.stack([f[:, :, -2:].swapaxes(1, 2) for f in fields])  4.34 us
    another operation x5, local copies, waits for them, and re-layouts, col_rims(): jnp.stack([f[:, :, :2].swapaxes(1, 2) for f in fields])  3.42 us
    ppermute x2, starting transfers between devices, padded_2(): after = lax.ppermute(leading, axis, down)  3.35 us
  transfers between devices with their start and end apart: 12, of which 2 were waited for; matrix products, arithmetic and copies ran while one was open for 22% of the time, Pallas kernels for 10%

commit v1 on v0

v1 whole, which is shorter than its diff:
```python
import functools
import jax
import jax.numpy as jnp
from jax import lax
from jax.experimental import pallas as pl
from jax.experimental.pallas import tpu as pltpu
from jax.sharding import PartitionSpec as P

ITERS = 4
LANES = 128
RIM = 8
LOW, HIGH = 0.2, 9.2
CENTRE, RADIUS = (HIGH + LOW) / 2, (HIGH - LOW) / 2
MESH = pl.DeviceIdType.MESH
F32 = jnp.float32


def put(out, k, value):
    out[k] = value if out[k] is None else out[k] + value


def times_operator(poly):
    out = [None] * (len(poly) + 1)
    for k, c in enumerate(poly):
        put(out, k, CENTRE * c)
        if k == 0:
            put(out, 1, RADIUS * c)
        else:
            half = (0.5 * RADIUS) * c
            put(out, k + 1, half)
            put(out, k - 1, half)
    return out


def inner(p, q, table):
    total = None
    for i, a in enumerate(p):
        part = None
        for j, b in enumerate(q):
            term = b * table[i][j]
            part = term if part is None else part + term
        part = a * part
        total = part if total is None else total + part
    return total


def add_scaled(p, scale, q):
    out = []
    for k in range(max(len(p), len(q))):
        if k >= len(p):
            out.append(scale * q[k])
        elif k >= len(q):
            out.append(p[k])
        else:
            out.append(p[k] + scale * q[k])
    return out


def weights_from(moments):
    table = [
        [
            moments[j] if i == 0 else moments[i] if j == 0 else 0.5 * (moments[i + j] + moments[abs(i - j)])
            for j in range(ITERS + 1)
        ]
        for i in range(ITERS)
    ]
    residual = [jnp.ones_like(moments[0])]
    direction = residual
    result = []
    norm_now = moments[0]
    for iteration in range(ITERS):
        image = times_operator(direction)
        step = norm_now / inner(direction, image, table)
        result = add_scaled(result, step, direction)
        if iteration + 1 < ITERS:
            residual = add_scaled(residual, -step, image)
            norm_next = inner(residual, residual, table)
            direction = add_scaled(residual, norm_next / norm_now, direction)
            norm_now = norm_next
    return result


def lane_index(rows):
    return lax.broadcasted_iota(jnp.int32, (rows, LANES), 1)


def roll(x, amount):
    return pltpu.roll(x, amount % LANES if isinstance(amount, int) else amount, 1)


def ahead(parts, by, lane):
    turned = [roll(p, -by) for p in parts] + [jnp.zeros_like(parts[0])]
    return [jnp.where(lane < LANES - by, turned[h], turned[h + 1]) for h in range(len(parts))]


def behind(parts, by, lane):
    turned = [jnp.zeros_like(parts[0])] + [roll(p, by) for p in parts]
    return [jnp.where(lane < by, turned[h], turned[h + 1]) for h in range(len(parts))]


def guarded(condition, action):
    @pl.when(condition)
    def _():
        action()


def kernel(
    sizes,
    theta_in, salt_in, vx_in, vy_in, land_in, kappa_in, forcing_in, bottom_in, theta_cot_in, salt_cot_in, surface_in,
    theta_grad, salt_grad, kappa_grad, forcing_grad,
    theta, salt, vx, vy, land, kappa, forcing, theta_cot, salt_cot,
    surface, bottom, wet, wet_after, first, second, open_y, inverse, link, ratio, theta_mix, salt_mix,
    theta_adj, salt_adj, k_fixed, k_zeta, zeta, seam_own, seam_left, seam_right, seam, slots,
    local_sem, rim_send, rim_recv, halo_send, halo_recv, sum_send, sum_recv,
):
    depth, rows, cols = sizes
    halves = cols // LANES
    top, end = RIM, RIM + rows
    mesh_rows, mesh_cols = lax.axis_size("trow"), lax.axis_size("tcol")
    count = mesh_rows * mesh_cols
    row, col = lax.axis_index("trow"), lax.axis_index("tcol")
    has_before, has_after = row > 0, row < mesh_rows - 1
    has_left, has_right = col > 0, col < mesh_cols - 1
    lane = lane_index(rows)
    spot = ((lane + 2) & 3) - 2

    def at(f, h, k):
        return (f * halves + h) * depth + k

    surface[...] = jnp.zeros_like(surface)
    bottom[...] = jnp.zeros_like(bottom)
    seam_left[...] = jnp.zeros_like(seam_left)
    seam_right[...] = jnp.zeros_like(seam_right)

    started = []

    def fetch(src, dst):
        copy = pltpu.make_async_copy(src, dst, local_sem.at[len(started)])
        copy.start()
        started.append(copy)
        return copy

    middle = pl.ds(LANES, cols)
    get_surface = fetch(surface_in, surface.at[pl.ds(RIM, rows), middle])
    get_bottom = fetch(bottom_in, bottom.at[pl.ds(RIM, rows), middle])

    def fetch_halves(src, dst):
        return [
            fetch(src.at[:, :, pl.ds(h * LANES, LANES)], dst.at[pl.ds(h * src.shape[0], src.shape[0])])
            for h in range(halves)
        ]

    get_land = fetch_halves(land_in, land)
    get_theta = fetch_halves(theta_in, theta)
    get_salt = fetch_halves(salt_in, salt)
    get_vx = fetch_halves(vx_in, vx)
    get_vy = fetch_halves(vy_in, vy)
    get_kappa = fetch_halves(kappa_in, kappa)
    get_theta_cot = fetch_halves(theta_cot_in, theta_cot)
    get_salt_cot = fetch_halves(salt_cot_in, salt_cot)
    get_forcing = fetch(forcing_in, forcing)

    def arrived(copies):
        for copy in copies:
            copy.wait()

    barrier = pltpu.get_barrier_semaphore()

    def other(i):
        return (lax.rem(row + lax.div(i, mesh_cols), mesh_rows), lax.rem(col + lax.rem(i, mesh_cols), mesh_cols))

    def greet(i, carry):
        pl.semaphore_signal(barrier, inc=1, device_id=other(i), device_id_type=MESH)
        return carry

    lax.fori_loop(1, count, greet, 0)
    pl.semaphore_wait(barrier, count - 1)

    rims = []
    for dr in (-1, 0, 1):
        for dc in (-1, 0, 1):
            if dr == 0 and dc == 0:
                continue
            conditions = [has_before] * (dr < 0) + [has_after] * (dr > 0) + [has_left] * (dc < 0) + [has_right] * (dc > 0)
            sources = [has_after] * (dr < 0) + [has_before] * (dr > 0) + [has_right] * (dc < 0) + [has_left] * (dc > 0)
            src_rows = pl.ds(0, RIM) if dr < 0 else pl.ds(rows - RIM, RIM) if dr > 0 else pl.ds(0, rows)
            src_cols = pl.ds(0, LANES) if dc < 0 else pl.ds(cols - LANES, LANES) if dc > 0 else pl.ds(0, cols)
            dst_rows = pl.ds(end, RIM) if dr < 0 else pl.ds(0, RIM) if dr > 0 else pl.ds(top, rows)
            dst_cols = pl.ds(LANES + cols, LANES) if dc < 0 else pl.ds(0, LANES) if dc > 0 else middle
            for src, dst in ((surface_in, surface), (bottom_in, bottom)):
                i = len(rims)
                copy = pltpu.make_async_remote_copy(
                    src_ref=src.at[src_rows, src_cols],
                    dst_ref=dst.at[dst_rows, dst_cols],
                    send_sem=rim_send.at[i],
                    recv_sem=rim_recv.at[i],
                    device_id=(row + dr, col + dc),
                    device_id_type=MESH,
                )
                rims.append((copy, functools.reduce(jnp.logical_and, conditions), functools.reduce(jnp.logical_and, sources)))
    for copy, sends, _ in rims:
        guarded(sends, copy.start)

    arrived([get_bottom] + get_land)

    def wet_level(k, carry):
        for h in range(halves):
            depth_here = bottom[top:end, LANES * (h + 1) : LANES * (h + 2)]
            value = jnp.where(k < depth_here, land[h * depth + k].astype(F32), 0.0)
            wet[h * depth + k, 0:rows] = value
            wet[h * depth + k, rows : rows + RIM] = jnp.ones((RIM, LANES), F32)
        return carry

    lax.fori_loop(0, depth, wet_level, 0)

    def wet_at(h, k):
        return wet[h * depth + k, 0:rows]

    arrived(get_theta + get_salt + get_vx + get_vy)

    def pack(k, parts, packed):
        both = jnp.where(lane < LANES // 2, parts[0], parts[-1])
        here = ((lane + 2 - 4 * k) & (LANES - 1)) < 4
        return jnp.where(here, roll(both, 4 * k), packed)

    def prepare(k, packs):
        wets = [wet_at(h, k) for h in range(halves)]
        wets_ahead = ahead(wets, 1, lane)
        qt, qs, uy = [], [], []
        for h in range(halves):
            i = h * depth + k
            qt.append(theta[i] * wets[h])
            qs.append(salt[i] * wets[h])
            uy.append(vy[i])
            first[at(0, h, k), top:end] = qt[h]
            first[at(1, h, k), top:end] = qs[h]
            first[at(2, h, k), top:end] = vx[i] * wets[h] * wet[i, 1 : rows + 1] * (1.0 / 12.0)
            open_y[i] = uy[h] * wets[h] * wets_ahead[h] * (1.0 / 12.0)
        return tuple(pack(k, parts, packed) for parts, packed in zip((qt, qs, uy, wets), packs))

    blank = jnp.zeros((rows, LANES), F32)
    for f, packed in enumerate(lax.fori_loop(0, depth, prepare, (blank,) * 4)):
        seam_own[f] = packed

    def remote(src, dst, i, device):
        return pltpu.make_async_remote_copy(
            src_ref=src, dst_ref=dst, send_sem=halo_send.at[i], recv_sem=halo_recv.at[i], device_id=device, device_id_type=MESH
        )

    after, before = (row + 1, col), (row - 1, col)
    right, left = (row, col + 1), (row, col - 1)
    both_tracers = pl.ds(0, 3 * halves * depth)
    stage_one = [
        (remote(first.at[both_tracers, pl.ds(end - 2, 2)], first.at[both_tracers, pl.ds(top - 2, 2)], 0, after), has_after, has_before),
        (remote(first.at[both_tracers, pl.ds(top, 2)], first.at[both_tracers, pl.ds(end, 2)], 1, before), has_before, has_after),
        (remote(wet.at[:, pl.ds(0, 1)], wet_after.at[:, pl.ds(0, 1)], 2, before), has_before, has_after),
        (remote(seam_own.at[pl.ds(0, 4)], seam_left.at[pl.ds(0, 4)], 3, right), has_right, has_left),
        (remote(seam_own.at[pl.ds(0, 4)], seam_right.at[pl.ds(0, 4)], 4, left), has_left, has_right),
    ]
    for copy, sends, _ in stage_one:
        guarded(sends, copy.start)

    def clear(missing, ref, start):
        @pl.when(missing)
        def _():
            def one(i, carry):
                ref[i, start : start + 2] = jnp.zeros((2, LANES), F32)
                return carry

            lax.fori_loop(0, ref.shape[0], one, 0)

    for ref in (first, second):
        clear(jnp.logical_not(has_before), ref, top - 2)
        clear(jnp.logical_not(has_after), ref, end)
    clear(jnp.logical_not(has_after), wet_after, 0)

    get_surface.wait()
    for copy, _, receives in rims:
        guarded(receives, copy.wait_recv)
    wide = (rows + 2 * RIM, cols + 2 * LANES)
    row_at = lax.broadcasted_iota(jnp.int32, wide, 0) - RIM + row * rows
    col_at = lax.broadcasted_iota(jnp.int32, wide, 1) - LANES + col * cols
    inside = ((row_at >= 0) & (row_at < rows * mesh_rows)) & ((col_at >= 0) & (col_at < cols * mesh_cols))
    scaled = (bottom[...].astype(F32) * (1.0 / depth) + (4.2 - CENTRE)) * (1.0 / RADIUS)
    basis = [surface[...]]
    for k in range(ITERS):
        field = basis[-1]
        beside = (pltpu.roll(field, 1, 0) + pltpu.roll(field, wide[0] - 1, 0)) + (
            pltpu.roll(field, 1, 1) + pltpu.roll(field, wide[1] - 1, 1)
        )
        image = scaled * field - beside * (1.0 / RADIUS)
        if k > 0:
            image = 2.0 * image - basis[-2]
        basis.append(jnp.where(inside, image, 0.0))

    def own_product(a, b):
        product = basis[a][top:end, LANES : LANES + cols] * basis[b][top:end, LANES : LANES + cols]
        tiles = [
            product[i : i + 8, j : j + LANES] for i in range(0, rows, 8) for j in range(0, cols, LANES)
        ]
        return functools.reduce(jnp.add, tiles)

    partial = [own_product(a, b) for a, b in ((0, 0), (0, 1), (0, 2), (0, 3), (0, 4), (2, 3), (3, 3), (3, 4))]
    small_lane = lane_index(8)
    width = LANES // 2
    while len(partial) > 1:
        folded = [p + pltpu.roll(p, LANES - width, 1) for p in partial]
        half = len(folded) // 2
        take_first = (small_lane & (2 * width - 1)) < width
        partial = [
            jnp.where(take_first, folded[i], pltpu.roll(folded[i + half], width, 1)) for i in range(half)
        ]
        width //= 2
    slots[0:1] = jnp.sum(partial[0], axis=0, keepdims=True)

    def sum_copy(i):
        return pltpu.make_async_remote_copy(
            src_ref=slots.at[pl.ds(0, 1)],
            dst_ref=slots.at[pl.ds(i, 1)],
            send_sem=sum_send.at[i],
            recv_sem=sum_recv.at[i],
            device_id=other(i),
            device_id_type=MESH,
        )

    def send_sum(i, carry):
        sum_copy(i).start()
        return carry

    lax.fori_loop(1, count, send_sum, 0)
    for k in range(ITERS):
        for h in range(halves + 2):
            zeta[k, h] = basis[k][:, h * LANES : (h + 1) * LANES]

    arrived(get_kappa + get_theta_cot + get_salt_cot)

    def couple_at(h, k):
        return kappa[h * (depth - 1) + k] * wet_at(h, k) * wet_at(h, k + 1)

    def down_level(k, couples, carry):
        out = []
        for h in range(halves):
            num, den, couple_before, yt, ys, yw = carry[h]
            i = h * depth + k
            den_next = num + couples[h] * den if couples is not None else num
            num_next = den_next + couples[h] * num if couples is not None else num
            inv = den * (1.0 / den_next)
            lower = couple_before * inv
            inverse[i] = inv
            link[i] = lower
            if couples is not None:
                ratio[i] = couples[h] * inv
            yt = theta_cot[i] * inv + lower * yt
            ys = salt_cot[i] * inv + lower * ys
            yw = wet_at(h, k) * inv + lower * yw
            second[at(0, h, k), top:end] = yt
            second[at(1, h, k), top:end] = ys
            second[at(2, h, k), top:end] = yw
            out.append((num_next, den_next, couples[h] if couples is not None else couple_before, yt, ys, yw))
        return tuple(out)

    one = jnp.ones((rows, LANES), F32)
    carry = ((one, one, blank, blank, blank, blank),) * halves
    carry = lax.fori_loop(0, depth - 1, lambda k, c: down_level(k, [couple_at(h, k) for h in range(halves)], c), carry)
    carry = down_level(depth - 1, None, carry)

    def up_level(i, carry):
        k = depth - 2 - i
        values, packs = carry
        new = []
        for f in range(3):
            parts = []
            for h in range(halves):
                x = second[at(f, h, k), top:end] + ratio[h * depth + k] * values[f][h]
                second[at(f, h, k), top:end] = x
                parts.append(x)
            new.append(tuple(parts))
        return tuple(new), tuple(pack(k, new[f], packs[f]) for f in range(3))

    last = tuple(tuple(carry[h][3 + f] for h in range(halves)) for f in range(3))
    packs = tuple(pack(depth - 1, last[f], blank) for f in range(3))
    _, packs = lax.fori_loop(0, depth - 1, up_level, (last, packs))
    for f in range(3):
        seam_own[4 + f] = packs[f]
    stage_two = [
        (remote(second.at[:, pl.ds(end - 2, 2)], second.at[:, pl.ds(top - 2, 2)], 5, after), has_after, has_before),
        (remote(second.at[:, pl.ds(top, 2)], second.at[:, pl.ds(end, 2)], 6, before), has_before, has_after),
        (remote(seam_own.at[pl.ds(4, 3)], seam_left.at[pl.ds(4, 3)], 7, right), has_right, has_left),
        (remote(seam_own.at[pl.ds(4, 3)], seam_right.at[pl.ds(4, 3)], 8, left), has_left, has_right),
    ]
    for copy, sends, _ in stage_two:
        guarded(sends, copy.start)

    for copy, sends, receives in stage_one:
        guarded(sends, copy.wait_send)
        guarded(receives, copy.wait_recv)

    def close_faces(i, carry):
        first[2 * halves * depth + i, top - 1 : top] = first[2 * halves * depth + i, top - 1 : top] * wet[i, 0:1]
        first[2 * halves * depth + i, end - 1 : end] = first[2 * halves * depth + i, end - 1 : end] * wet_after[i, 0:1]
        return carry

    lax.fori_loop(0, halves * depth, close_faces, 0)

    def across_left(f):
        return jnp.where(spot < 0, seam_left[f], seam_own[f])

    def across_right(f):
        return jnp.where(spot < 0, seam_own[f], seam_right[f])

    wet_left, wet_right = across_left(3), across_right(3)
    open_left = across_left(2) * wet_left * roll(wet_left, -1) * (1.0 / 12.0)
    open_right = across_right(2) * wet_right * roll(wet_right, -1) * (1.0 / 12.0)

    def forward_seam(f):
        q = across_left(f)
        flux = open_left * (7.0 * (q + roll(q, -1)) - roll(q, 1) - roll(q, -2))
        flux = jnp.where(spot == -1, flux, 0.0)
        cross = jnp.where(spot == 0, open_left * roll(q, 1), 0.0)
        at_left = roll(flux, 1) + cross - roll(cross, 1)
        q = across_right(f)
        flux = open_right * (7.0 * (q + roll(q, -1)) - roll(q, 1) - roll(q, -2))
        flux = jnp.where(spot == -1, flux, 0.0)
        cross = jnp.where(spot == -2, open_right * roll(q, -2), 0.0)
        at_right = cross - flux - roll(cross, 1)
        return jnp.where(spot >= 0, at_left, at_right)

    def adjoint_seam(m_left, m_right):
        faces = jnp.where(spot < 0, open_left * (m_left - roll(m_left, -1)), 0.0)
        at_left = 7.0 * roll(faces, 1) - roll(faces, 2)
        faces = jnp.where((spot == -1) | (spot == 0), open_right * (m_right - roll(m_right, -1)), 0.0)
        at_right = 7.0 * faces - roll(faces, -1)
        return jnp.where(spot >= 0, at_left, jnp.where(spot == -2, -roll(faces, -1), at_right))

    def unpack(k, f):
        turned = roll(seam[f], LANES - 4 * k)
        parts = [None] * halves
        parts[0] = jnp.where(lane < 2, turned, 0.0)
        parts[-1] = jnp.where(lane >= LANES - 2, turned, 0.0)
        return parts

    seam[0] = forward_seam(0)
    seam[1] = forward_seam(1)
    get_forcing.wait()
    for h in range(halves):
        theta[h * depth] = theta[h * depth] + forcing[:, h * LANES : (h + 1) * LANES] * wet_at(h, 0)

    def advected(k, f, raw):
        centre = [first[at(f, h, k), top:end] for h in range(halves)]
        next_one, next_two, previous = ahead(centre, 1, lane), ahead(centre, 2, lane), behind(centre, 1, lane)
        fluxes = [
            open_y[h * depth + k] * (7.0 * (centre[h] + next_one[h]) - previous[h] - next_two[h]) for h in range(halves)
        ]
        fluxes_before = behind(fluxes, 1, lane)
        edges = unpack(k, f)
        out = []
        for h in range(halves):
            q = [first[at(f, h, k), top + s : end + s] for s in (-2, -1, 0, 1, 2)]
            here = first[at(2, h, k), top:end] * (7.0 * (q[2] + q[3]) - q[1] - q[4])
            ahead_of = first[at(2, h, k), top - 1 : end - 1] * (7.0 * (q[1] + q[2]) - q[0] - q[3])
            value = raw[h * depth + k] - (here - ahead_of) - (fluxes[h] - fluxes_before[h])
            out.append(value if edges[h] is None else value + edges[h])
        return out

    def forward_down(k, carry):
        adv_t, adv_s = advected(k, 0, theta), advected(k, 1, salt)
        out = []
        for h in range(halves):
            i = h * depth + k
            yt = adv_t[h] * inverse[i] + link[i] * carry[h][0]
            ys = adv_s[h] * inverse[i] + link[i] * carry[h][1]
            theta_mix[i] = yt
            salt_mix[i] = ys
            out.append((yt, ys))
        return tuple(out)

    carry = lax.fori_loop(0, depth, forward_down, ((blank, blank),) * halves)

    def forward_up(n, carry):
        k = depth - 2 - n
        out = []
        for h in range(halves):
            i = h * depth + k
            xt = theta_mix[i] + ratio[i] * carry[h][0]
            xs = salt_mix[i] + ratio[i] * carry[h][1]
            dt, ds = xt - carry[h][0], xs - carry[h][1]
            at_, as_, aw = [
                second[at(f, h, k), top:end] - second[at(f, h, k + 1), top:end] for f in range(3)
            ]
            closed = -wet_at(h, k) * wet_at(h, k + 1)
            k_fixed[i] = closed * (at_ * dt + as_ * ds)
            k_zeta[i] = closed * aw * (0.2 * dt - 0.15 * ds)
            out.append((xt, xs))
        return tuple(out)

    lax.fori_loop(0, depth - 1, forward_up, carry)

    for copy, sends, receives in stage_two:
        guarded(receives, copy.wait_recv)
    seam[0] = adjoint_seam(across_left(4), across_right(4))
    seam[1] = adjoint_seam(across_left(5), across_right(5))

    def adjoint_level(k, windows, edges):
        centre = [windows[h][2] for h in range(halves)]
        nexts = ahead(centre, 1, lane)
        faces = [open_y[h * depth + k] * (centre[h] - nexts[h]) for h in range(halves)]
        face_next, face_one, face_two = ahead(faces, 1, lane), behind(faces, 1, lane), behind(faces, 2, lane)
        out = []
        for h in range(halves):
            m = windows[h]
            hx = [first[at(2, h, k), top + s : end + s] * (m[s + 2] - m[s + 3]) for s in (-2, -1, 0, 1)]
            change = 7.0 * ((hx[2] + hx[1]) + (faces[h] + face_one[h])) - (hx[3] + hx[0]) - (face_next[h] + face_two[h])
            if edges[h] is not None:
                change = change + edges[h]
            out.append(centre[h] - wet_at(h, k) * change)
        return out

    def adjoint_fixed(k, carry):
        for f, target in ((0, theta_adj), (1, salt_adj)):
            windows = [
                [second[at(f, h, k), top + s : end + s] for s in (-2, -1, 0, 1, 2)] for h in range(halves)
            ]
            result = adjoint_level(k, windows, unpack(k, f))
            for h in range(halves):
                target[h * depth + k] = result[h]
        return carry

    lax.fori_loop(0, depth, adjoint_fixed, 0)

    def got_sum(i, carry):
        sum_copy(i).wait_recv()
        return carry

    lax.fori_loop(1, count, got_sum, 0)
    total = jnp.sum(slots[...], axis=0, keepdims=True)
    for step in (8, 4, 2, 1):
        total = total + pltpu.roll(total, LANES - step, 1)
    m = [jnp.broadcast_to(total[:, 16 * g : 16 * g + 1], (8, LANES)) for g in range(8)]
    m = m[:5] + [2.0 * m[5] - m[1], 2.0 * m[6] - m[0], 2.0 * m[7] - m[1]]
    weights = [jnp.concatenate([w] * (wide[0] // 8), axis=0) for w in weights_from(m)]
    for h in range(halves + 2):
        zeta[0, h] = (weights[0] * zeta[0, h] + weights[1] * zeta[1, h]) + (weights[2] * zeta[2, h] + weights[3] * zeta[3, h])

    def everywhere(outer, inner_part):
        value = jnp.where(lane >= LANES - 2, outer, jnp.where(lane < 2, inner_part, 0.0))
        for step in (4, 8, 16, 32, 64):
            value = value + roll(value, step)
        return value

    zeta_left = everywhere(zeta[0, 0, top:end], zeta[0, 1, top:end])
    zeta_right = everywhere(zeta[0, halves, top:end], zeta[0, halves + 1, top:end])
    seam[0] = adjoint_seam(across_left(6) * zeta_left, across_right(6) * zeta_right)

    def finish(k, carry):
        windows = [
            [second[at(2, h, k), top + s : end + s] * zeta[0, h + 1, top + s : end + s] for s in (-2, -1, 0, 1, 2)]
            for h in range(halves)
        ]
        result = adjoint_level(k, windows, unpack(k, 0))
        for h in range(halves):
            i = h * depth + k
            theta_grad[k, :, h * LANES : (h + 1) * LANES] = theta_adj[i] + 0.2 * result[h]
            salt_grad[k, :, h * LANES : (h + 1) * LANES] = salt_adj[i] - 0.15 * result[h]
        return carry

    lax.fori_loop(0, depth, finish, 0)

    def finish_kappa(k, carry):
        for h in range(halves):
            i = h * depth + k
            kappa_grad[k, :, h * LANES : (h + 1) * LANES] = k_fixed[i] + k_zeta[i] * zeta[0, h + 1, top:end]
        return carry

    lax.fori_loop(0, depth - 1, finish_kappa, 0)
    for h in range(halves):
        z = zeta[0, h + 1, top:end]
        theta_top = second[at(0, h, 0), top:end] + 0.2 * z * second[at(2, h, 0), top:end]
        forcing_grad[:, h * LANES : (h + 1) * LANES] = z + wet_at(h, 0) * theta_top

    for copy, sends, _ in rims + stage_two:
        guarded(sends, copy.wait_send)

    def sent_sum(i, carry):
        sum_copy(i).wait_send()
        return carry

    lax.fori_loop(1, count, sent_sum, 0)


def shards(*args):
    theta, bottom = args[0], args[7]
    depth, rows, cols = theta.shape
    halves = cols // LANES
    count = lax.axis_size("trow") * lax.axis_size("tcol")
    tall = rows + 2 * RIM
    V = pltpu.VMEM
    DMA = pltpu.SemaphoreType.DMA
    flat = V((halves * depth, rows, LANES), F32)
    ints = V((halves * depth, rows, LANES), jnp.int32)
    upper = V((halves * (depth - 1), rows, LANES), F32)
    tile = V((7, rows, LANES), F32)
    scratch = [
        flat, flat, flat, flat, ints, upper, V((rows, cols), F32), flat, flat,
        V((tall, cols + 2 * LANES), F32), V((tall, cols + 2 * LANES), jnp.int32),
        V((halves * depth, rows + RIM, LANES), F32), V((halves * depth, RIM, LANES), F32),
        V((3 * halves * depth, tall, LANES), F32), V((3 * halves * depth, tall, LANES), F32),
        flat, flat, flat, flat, flat, flat, flat, flat, flat, flat,
        V((ITERS, halves + 2, tall, LANES), F32), tile, tile, tile, V((2, rows, LANES), F32),
        V((count, LANES), F32),
        DMA((3 + 8 * halves,)), DMA((16,)), DMA((16,)), DMA((9,)), DMA((9,)), DMA((count,)), DMA((count,)),
    ]
    outs = [(depth, rows, cols), (depth, rows, cols), (depth - 1, rows, cols), (rows, cols)]
    return tuple(
        pl.pallas_call(
            functools.partial(kernel, (depth, rows, cols)),
            out_shape=[jax.ShapeDtypeStruct(o, F32) for o in outs],
            in_specs=[pl.BlockSpec(memory_space=pltpu.HBM)] * len(args),
            out_specs=[pl.BlockSpec(memory_space=pltpu.VMEM)] * len(outs),
            scratch_shapes=scratch,
            compiler_params=pltpu.CompilerParams(
                collective_id=0, has_side_effects=True, vmem_limit_bytes=48 * 1024 * 1024
            ),
        )(*[pltpu.with_memory_space_constraint(a, pltpu.HBM) for a in args])
    )


def solution(mesh):
    cube, plane = P(None, "trow", "tcol"), P("trow", "tcol")
    in_specs = (cube,) * 6 + (plane,) * 2 + (cube,) * 2 + (plane,)
    out_specs = (cube,) * 3 + (plane,)
    return jax.shard_map(shards, mesh=mesh, in_specs=in_specs, out_specs=out_specs, check_vma=False)
```

time: 129 us -> 35.4 us (0.27)
  the two profiles are of different devices: /device:TPU:1 before, /device:TPU:0 now
where the time goes in v1:
time: 35.4 us; the launch traced here: 35.3 us
  Pallas kernels  31.8 us (90%)
  local copies, waits for them, and re-layouts  2.86 us (8%)
  between operations  0.64 us (2%)
    pallas_call x1, Pallas kernels, shards(): pl.pallas_call(functools.partial(kernel, (depth, rows, cols)), out_shape=...  31.8 us
    unnamed x4, local copies, waits for them, and re-layouts  2.86 us

profile of v1, /device:TPU:0, one launch (start us, length us, event | category | flops | bytes accessed | tf_op | source)
XLA Modules:
  0.0 35.3 jit_solution(7470347120473420886)
XLA Ops:
  0.6 31.8 %shard_map.138 = (f32[25,16,256]{2,1,0:T(8,128)S(1)}, f32[25,16,256]{2,1,0:T(8,128)S(1)}, f32[24,16,256]{2,1,0:T(8,128)S(1)}, f32[16,256]{1,0:T(8,128)S(1)}) custom-call(f32[25,16,256]{2,1,0:T(8,128)} %theta_in.1, f32[25,16,256]{2,1,0:T(8,128)} %salt_in.1, f32[25,16,256]{2,1,0:T(8,128)} %vx_in.1, f32[25,16,256]{2,1,0:T(8,128)} %vy_in.1, ...), custom_call_target="tpu_custom_call" | custom-call | tf_op jit(solution)/shard_map/pallas_call | solution.py:614
  32.4 0.8 %copy.19 = f32[25,16,256]{2,1,0:T(8,128)} copy(f32[25,16,256]{2,1,0:T(8,128)S(1)} %get-tuple-element.8) | data formatting | bytes 819200
  33.2 0.8 %copy.20 = f32[25,16,256]{2,1,0:T(8,128)} copy(f32[25,16,256]{2,1,0:T(8,128)S(1)} %get-tuple-element.9) | data formatting | bytes 819200
  33.9 0.7 %copy.21 = f32[24,16,256]{2,1,0:T(8,128)} copy(f32[24,16,256]{2,1,0:T(8,128)S(1)} %get-tuple-element.10) | data formatting | bytes 786432
  34.7 0.6 %copy.22 = f32[16,256]{1,0:T(8,128)} copy(f32[16,256]{1,0:T(8,128)S(1)} %get-tuple-element.11) | data formatting | bytes 32768

commit v2 on v1

v2 whole, which is shorter than its diff:
```python
import functools
import jax
import jax.numpy as jnp
from jax import lax
from jax.experimental import pallas as pl
from jax.experimental.pallas import tpu as pltpu
from jax.sharding import PartitionSpec as P

ITERS = 4
LANES = 128
RIM = 8
LOW, HIGH = 0.2, 9.2
CENTRE, RADIUS = (HIGH + LOW) / 2, (HIGH - LOW) / 2
MESH = pl.DeviceIdType.MESH
F32 = jnp.float32


def put(out, k, value):
    out[k] = value if out[k] is None else out[k] + value


def times_operator(poly):
    out = [None] * (len(poly) + 1)
    for k, c in enumerate(poly):
        put(out, k, CENTRE * c)
        if k == 0:
            put(out, 1, RADIUS * c)
        else:
            half = (0.5 * RADIUS) * c
            put(out, k + 1, half)
            put(out, k - 1, half)
    return out


def inner(p, q, table):
    total = None
    for i, a in enumerate(p):
        part = None
        for j, b in enumerate(q):
            term = b * table[i][j]
            part = term if part is None else part + term
        part = a * part
        total = part if total is None else total + part
    return total


def add_scaled(p, scale, q):
    out = []
    for k in range(max(len(p), len(q))):
        if k >= len(p):
            out.append(scale * q[k])
        elif k >= len(q):
            out.append(p[k])
        else:
            out.append(p[k] + scale * q[k])
    return out


def weights_from(moments):
    table = [
        [
            moments[j] if i == 0 else moments[i] if j == 0 else 0.5 * (moments[i + j] + moments[abs(i - j)])
            for j in range(ITERS + 1)
        ]
        for i in range(ITERS)
    ]
    residual = [jnp.ones_like(moments[0])]
    direction = residual
    result = []
    norm_now = moments[0]
    for iteration in range(ITERS):
        image = times_operator(direction)
        step = norm_now / inner(direction, image, table)
        result = add_scaled(result, step, direction)
        if iteration + 1 < ITERS:
            residual = add_scaled(residual, -step, image)
            norm_next = inner(residual, residual, table)
            direction = add_scaled(residual, norm_next / norm_now, direction)
            norm_now = norm_next
    return result


def lane_index(rows):
    return lax.broadcasted_iota(jnp.int32, (rows, LANES), 1)


def roll(x, amount):
    return pltpu.roll(x, amount % LANES if isinstance(amount, int) else amount & (LANES - 1), 1)


def shifted(parts, rim, k, by, lane):
    if by > 0:
        turned = [roll(p, -by) for p in parts] + [roll(rim, LANES - 4 * k - by)]
        edge = LANES - by
    else:
        turned = [roll(rim, LANES - 4 * k - by)] + [roll(p, -by) for p in parts]
        edge = -by
    return [jnp.where(lane < edge, turned[h], turned[h + 1]) for h in range(len(parts))]


def by_groups(start, stop, group, body, carry):
    count = (stop - start) // group
    carry = lax.fori_loop(0, count, lambda i, c: body([start + i * group + u for u in range(group)], c), carry)
    rest = list(range(start + count * group, stop))
    return body(rest, carry) if rest else carry


def guarded(condition, action):
    @pl.when(condition)
    def _():
        action()


def solve_kernel(
    sizes,
    theta_in, salt_in, vx_in, vy_in, land_in, kappa_in, forcing_in, bottom_in, theta_cot_in, salt_cot_in, surface_in,
    cross, theta_adj, salt_adj, k_fixed, k_zeta, zeta, top_parts, sums,
    theta, salt, vx, vy, land, kappa, forcing, theta_cot, salt_cot,
    surface, bottom, wet, wet_after, first, second, open_y, inverse, link, ratio, theta_mix, salt_mix,
    seam_own, seam_left, seam_right, rim, slots,
    local_sem, rim_send, rim_recv, halo_send, halo_recv, sum_send, sum_recv,
):
    depth, rows, cols = sizes
    halves = cols // LANES
    top, end = RIM, RIM + rows
    mesh_rows, mesh_cols = lax.axis_size("trow"), lax.axis_size("tcol")
    count = mesh_rows * mesh_cols
    row, col = lax.axis_index("trow"), lax.axis_index("tcol")
    has_before, has_after = row > 0, row < mesh_rows - 1
    has_left, has_right = col > 0, col < mesh_cols - 1
    lane = lane_index(rows)
    spot = ((lane + 2) & 3) - 2
    blank = jnp.zeros((rows, LANES), F32)
    span = range(halves)

    def at(f, h, k):
        return (f * halves + h) * depth + k

    surface[...] = jnp.zeros_like(surface)
    bottom[...] = jnp.zeros_like(bottom)
    seam_left[...] = jnp.zeros_like(seam_left)
    seam_right[...] = jnp.zeros_like(seam_right)

    barrier = pltpu.get_barrier_semaphore()

    def others(action):
        for dc in range(1, mesh_cols):
            action(dc, (row, lax.rem(col + dc, mesh_cols)))

        def one_row(dr, carry):
            there = lax.rem(row + dr, mesh_rows)
            for dc in range(mesh_cols):
                action(dr * mesh_cols + dc, (there, lax.rem(col + dc, mesh_cols)))
            return carry

        lax.fori_loop(1, mesh_rows, one_row, 0)

    others(lambda i, device: pl.semaphore_signal(barrier, inc=1, device_id=device, device_id_type=MESH))

    started = []

    def fetch(src, dst):
        copy = pltpu.make_async_copy(src, dst, local_sem.at[len(started)])
        copy.start()
        started.append(copy)
        return copy

    middle = pl.ds(LANES, cols)
    get_surface = fetch(surface_in, surface.at[pl.ds(RIM, rows), middle])
    get_bottom = fetch(bottom_in, bottom.at[pl.ds(RIM, rows), middle])

    def fetch_halves(src, dst):
        return [
            fetch(src.at[:, :, pl.ds(h * LANES, LANES)], dst.at[pl.ds(h * src.shape[0], src.shape[0])]) for h in span
        ]

    get_land = fetch_halves(land_in, land)
    get_theta = fetch_halves(theta_in, theta)
    get_salt = fetch_halves(salt_in, salt)
    get_vx = fetch_halves(vx_in, vx)
    get_vy = fetch_halves(vy_in, vy)
    get_kappa = fetch_halves(kappa_in, kappa)
    get_theta_cot = fetch_halves(theta_cot_in, theta_cot)
    get_salt_cot = fetch_halves(salt_cot_in, salt_cot)
    get_forcing = fetch(forcing_in, forcing)

    def arrived(copies):
        for copy in copies:
            copy.wait()

    pl.semaphore_wait(barrier, count - 1)

    rims = []
    for dr in (-1, 0, 1):
        for dc in (-1, 0, 1):
            if dr == 0 and dc == 0:
                continue
            targets = [has_before] * (dr < 0) + [has_after] * (dr > 0) + [has_left] * (dc < 0) + [has_right] * (dc > 0)
            sources = [has_after] * (dr < 0) + [has_before] * (dr > 0) + [has_right] * (dc < 0) + [has_left] * (dc > 0)
            src_rows = pl.ds(0, RIM) if dr < 0 else pl.ds(rows - RIM, RIM) if dr > 0 else pl.ds(0, rows)
            src_cols = pl.ds(0, LANES) if dc < 0 else pl.ds(cols - LANES, LANES) if dc > 0 else pl.ds(0, cols)
            dst_rows = pl.ds(end, RIM) if dr < 0 else pl.ds(0, RIM) if dr > 0 else pl.ds(top, rows)
            dst_cols = pl.ds(LANES + cols, LANES) if dc < 0 else pl.ds(0, LANES) if dc > 0 else middle
            for src, dst in ((surface_in, surface), (bottom_in, bottom)):
                i = len(rims)
                copy = pltpu.make_async_remote_copy(
                    src_ref=src.at[src_rows, src_cols],
                    dst_ref=dst.at[dst_rows, dst_cols],
                    send_sem=rim_send.at[i],
                    recv_sem=rim_recv.at[i],
                    device_id=(row + dr, col + dc),
                    device_id_type=MESH,
                )
                rims.append((copy, functools.reduce(jnp.logical_and, targets), functools.reduce(jnp.logical_and, sources)))
    for copy, sends, _ in rims:
        guarded(sends, copy.start)

    arrived([get_bottom] + get_land)

    def wet_levels(levels, carry):
        for k in levels:
            for h in span:
                depth_here = bottom[top:end, LANES * (h + 1) : LANES * (h + 2)]
                wet[h * depth + k, 0:rows] = jnp.where(k < depth_here, land[h * depth + k].astype(F32), 0.0)
                wet[h * depth + k, rows : rows + RIM] = jnp.ones((RIM, LANES), F32)
        return carry

    by_groups(0, depth, 5, wet_levels, 0)

    def wet_at(h, k):
        return wet[h * depth + k, 0:rows]

    arrived(get_theta + get_salt + get_vx + get_vy)

    def pack(k, parts, packed):
        both = jnp.where(lane < LANES // 2, parts[0], parts[-1])
        here = ((lane + 2 - 4 * k) & (LANES - 1)) < 4
        return jnp.where(here, roll(both, 4 * k), packed)

    def prepare(levels, packs):
        for k in levels:
            wets = [wet_at(h, k) for h in span]
            qt, qs, uy = [], [], []
            for h in span:
                i = h * depth + k
                qt.append(theta[i] * wets[h])
                qs.append(salt[i] * wets[h])
                uy.append(vy[i])
                first[at(0, h, k), top:end] = qt[h]
                first[at(1, h, k), top:end] = qs[h]
                first[at(2, h, k), top:end] = vx[i] * wets[h] * wet[i, 1 : rows + 1] * (1.0 / 12.0)
            packs = tuple(pack(k, parts, packed) for parts, packed in zip((qt, qs, uy, wets), packs))
        return packs

    for f, packed in enumerate(by_groups(0, depth, 5, prepare, (blank,) * 4)):
        seam_own[f] = packed

    def remote(src, dst, i, device):
        return pltpu.make_async_remote_copy(
            src_ref=src, dst_ref=dst, send_sem=halo_send.at[i], recv_sem=halo_recv.at[i], device_id=device, device_id_type=MESH
        )

    after, before = (row + 1, col), (row - 1, col)
    right, left = (row, col + 1), (row, col - 1)
    low, high, below, above = pl.ds(end - 2, 2), pl.ds(top, 2), pl.ds(top - 2, 2), pl.ds(end, 2)
    stage_one = [
        (remote(first.at[:, low], first.at[:, below], 0, after), has_after, has_before),
        (remote(first.at[:, high], first.at[:, above], 1, before), has_before, has_after),
        (remote(wet.at[:, pl.ds(0, 1)], wet_after.at[:, pl.ds(0, 1)], 2, before), has_before, has_after),
        (remote(seam_own.at[pl.ds(0, 4)], seam_left.at[pl.ds(0, 4)], 3, right), has_right, has_left),
        (remote(seam_own.at[pl.ds(0, 4)], seam_right.at[pl.ds(0, 4)], 4, left), has_left, has_right),
    ]
    for copy, sends, _ in stage_one:
        guarded(sends, copy.start)

    def clear(missing, ref, start):
        @pl.when(missing)
        def _():
            ref[:, start : start + 2] = jnp.zeros((ref.shape[0], 2, LANES), F32)

    for ref in (first, second):
        clear(jnp.logical_not(has_before), ref, top - 2)
        clear(jnp.logical_not(has_after), ref, end)
    clear(jnp.logical_not(has_after), wet_after, 0)

    get_surface.wait()
    for copy, _, receives in rims:
        guarded(receives, copy.wait_recv)
    wide = (rows + 2 * RIM, cols + 2 * LANES)
    row_at = lax.broadcasted_iota(jnp.int32, wide, 0) - RIM + row * rows
    col_at = lax.broadcasted_iota(jnp.int32, wide, 1) - LANES + col * cols
    inside = ((row_at >= 0) & (row_at < rows * mesh_rows)) & ((col_at >= 0) & (col_at < cols * mesh_cols))
    scaled = (bottom[...].astype(F32) * (1.0 / depth) + (4.2 - CENTRE)) * (1.0 / RADIUS)
    basis = [surface[...]]
    for k in range(ITERS):
        field = basis[-1]
        beside = (pltpu.roll(field, 1, 0) + pltpu.roll(field, wide[0] - 1, 0)) + (
            pltpu.roll(field, 1, 1) + pltpu.roll(field, wide[1] - 1, 1)
        )
        image = scaled * field - beside * (1.0 / RADIUS)
        if k > 0:
            image = 2.0 * image - basis[-2]
        basis.append(jnp.where(inside, image, 0.0))

    def own_product(a, b):
        product = basis[a][top:end, LANES : LANES + cols] * basis[b][top:end, LANES : LANES + cols]
        tiles = [product[i : i + 8, j : j + LANES] for i in range(0, rows, 8) for j in range(0, cols, LANES)]
        return functools.reduce(jnp.add, tiles)

    partial = [own_product(a, b) for a, b in ((0, 0), (0, 1), (0, 2), (0, 3), (0, 4), (2, 3), (3, 3), (3, 4))]
    small_lane = lane_index(8)
    width = LANES // 2
    while len(partial) > 1:
        half = len(partial) // 2
        take_first = (small_lane & (2 * width - 1)) < width
        partial = [
            jnp.where(take_first, a + roll(a, -width), b + roll(b, width)) for a, b in zip(partial[:half], partial[half:])
        ]
        width //= 2
    slots[0:1] = jnp.sum(partial[0], axis=0, keepdims=True)

    def sum_copy(i, device):
        return pltpu.make_async_remote_copy(
            src_ref=slots.at[pl.ds(0, 1)],
            dst_ref=slots.at[pl.ds(i, 1)],
            send_sem=sum_send.at[i],
            recv_sem=sum_recv.at[i],
            device_id=device,
            device_id_type=MESH,
        )

    others(lambda i, device: sum_copy(i, device).start())
    for k in range(ITERS):
        for h in range(halves + 2):
            zeta[k * (halves + 2) + h] = basis[k][:, h * LANES : (h + 1) * LANES]

    arrived(get_kappa + get_theta_cot + get_salt_cot)

    def down_level(k, last, carry):
        out = []
        for h in span:
            num, den, couple_before, yt, ys, yw = carry[h]
            i = h * depth + k
            wet_here = wet_at(h, k)
            if last:
                den_next = num_next = num
                couple = couple_before
            else:
                couple = kappa[h * (depth - 1) + k] * wet_here * wet_at(h, k + 1)
                den_next = num + couple * den
                num_next = den_next + couple * num
            inv = den * (1.0 / den_next)
            lower = couple_before * inv
            inverse[i] = inv
            link[i] = lower
            if not last:
                ratio[i] = couple * inv
            yt = theta_cot[i] * inv + lower * yt
            ys = salt_cot[i] * inv + lower * ys
            yw = wet_here * inv + lower * yw
            second[at(0, h, k), top:end] = yt
            second[at(1, h, k), top:end] = ys
            second[at(2, h, k), top:end] = yw
            out.append((num_next, den_next, couple, yt, ys, yw))
        return tuple(out)

    def down(levels, carry):
        for k in levels:
            carry = down_level(k, False, carry)
        return carry

    one = jnp.ones((rows, LANES), F32)
    carry = by_groups(0, depth - 1, 4, down, ((one, one, blank, blank, blank, blank),) * halves)
    carry = down_level(depth - 1, True, carry)

    def up(steps, values):
        for n in steps:
            k = depth - 2 - n
            new = []
            for f in range(3):
                parts = []
                for h in span:
                    x = second[at(f, h, k), top:end] + ratio[h * depth + k] * values[f][h]
                    second[at(f, h, k), top:end] = x
                    parts.append(x)
                new.append(tuple(parts))
            values = tuple(new)
        return values

    by_groups(0, depth - 1, 4, up, tuple(tuple(carry[h][3 + f] for h in span) for f in range(3)))

    def pack_second(levels, packs):
        for k in levels:
            packs = tuple(pack(k, [second[at(f, h, k), top:end] for h in span], packs[f]) for f in range(3))
        return packs

    for f, packed in enumerate(by_groups(0, depth, 5, pack_second, (blank,) * 3)):
        seam_own[4 + f] = packed
    stage_two = [
        (remote(second.at[:, low], second.at[:, below], 5, after), has_after, has_before),
        (remote(second.at[:, high], second.at[:, above], 6, before), has_before, has_after),
        (remote(seam_own.at[pl.ds(4, 3)], seam_left.at[pl.ds(4, 3)], 7, right), has_right, has_left),
        (remote(seam_own.at[pl.ds(4, 3)], seam_right.at[pl.ds(4, 3)], 8, left), has_left, has_right),
    ]
    for copy, sends, _ in stage_two:
        guarded(sends, copy.start)

    for copy, sends, receives in stage_one:
        guarded(sends, copy.wait_send)
        guarded(receives, copy.wait_recv)
    faces = 2 * halves * depth
    first[faces:, top - 1 : top] = first[faces:, top - 1 : top] * wet[:, 0:1]
    first[faces:, end - 1 : end] = first[faces:, end - 1 : end] * wet_after[:, 0:1]

    def open_across(uy, near):
        return uy * near * roll(near, -1) * (1.0 / 12.0)

    inner_side = spot < 0
    rim[0] = jnp.where(inner_side, seam_left[0], seam_right[0])
    rim[1] = jnp.where(inner_side, seam_left[1], seam_right[1])
    rim[3] = jnp.where(inner_side, seam_left[3], seam_right[3])
    open_left = open_across(seam_left[2], jnp.where(inner_side, seam_left[3], seam_own[3]))
    open_right = open_across(seam_right[2], seam_right[3])
    rim[2] = jnp.where(inner_side, open_left, open_right)

    def open_columns(levels, carry):
        ahead = [shifted([wet_at(h, k) for h in span], rim[3], k, 1, lane) for k in levels]
        for k, wets_ahead in zip(levels, ahead):
            for h in span:
                i = h * depth + k
                open_y[i] = vy[i] * wet_at(h, k) * wets_ahead[h] * (1.0 / 12.0)
        return carry

    by_groups(0, depth, 5, open_columns, 0)
    get_forcing.wait()
    for h in span:
        theta[h * depth] = theta[h * depth] + forcing[:, h * LANES : (h + 1) * LANES] * wet_at(h, 0)

    def column_shifts(ref, f, k, edges):
        centre = [ref[at(f, h, k), top:end] for h in span]
        return {s: shifted(centre, edges, k, s, lane) for s in (-2, -1, 1, 2)}

    def face_shifts(k, steps):
        centre = [open_y[h * depth + k] for h in span]
        return {s: shifted(centre, rim[2], k, s, lane) for s in steps}

    def forward_down(levels, carry):
        moved = [(face_shifts(k, (-1,)), [column_shifts(first, f, k, rim[f]) for f in range(2)]) for k in levels]
        for k, (uy, turned) in zip(levels, moved):
            out = []
            for h in span:
                i = h * depth + k
                found = []
                for f, raw in ((0, theta), (1, salt)):
                    q = [first[at(f, h, k), top + s : end + s] for s in (-2, -1, 0, 1, 2)]
                    c = turned[f]
                    row_here = first[at(2, h, k), top:end] * (7.0 * (q[2] + q[3]) - (q[1] + q[4]))
                    row_back = first[at(2, h, k), top - 1 : end - 1] * (7.0 * (q[1] + q[2]) - (q[0] + q[3]))
                    col_here = open_y[i] * (7.0 * (q[2] + c[1][h]) - (c[-1][h] + c[2][h]))
                    col_back = uy[-1][h] * (7.0 * (c[-1][h] + q[2]) - (c[-2][h] + c[1][h]))
                    value = raw[i] - (row_here - row_back) - (col_here - col_back)
                    found.append(value * inverse[i] + link[i] * carry[h][f])
                theta_mix[i] = found[0]
                salt_mix[i] = found[1]
                out.append(tuple(found))
            carry = tuple(out)
        return carry

    carry = by_groups(0, depth, 5, forward_down, ((blank, blank),) * halves)

    def forward_up(steps, carry):
        for n in steps:
            k = depth - 2 - n
            out = []
            for h in span:
                i = h * depth + k
                xt = theta_mix[i] + ratio[i] * carry[h][0]
                xs = salt_mix[i] + ratio[i] * carry[h][1]
                dt, ds = xt - carry[h][0], xs - carry[h][1]
                step_t, step_s, step_w = [
                    second[at(f, h, k), top:end] - second[at(f, h, k + 1), top:end] for f in range(3)
                ]
                closed = -wet_at(h, k) * wet_at(h, k + 1)
                k_fixed[h * (depth - 1) + k] = closed * (step_t * dt + step_s * ds)
                k_zeta[h * (depth - 1) + k] = closed * step_w * (0.2 * dt - 0.15 * ds)
                out.append((xt, xs))
            carry = tuple(out)
        return carry

    by_groups(0, depth - 1, 4, forward_up, carry)

    for copy, _, receives in stage_two:
        guarded(receives, copy.wait_recv)
    for f in range(3):
        rim[4 + f] = jnp.where(inner_side, seam_left[4 + f], seam_right[4 + f])

    def arms(u, wets):
        v = [wets * x for x in u]
        back, here = 7.0 * v[1], 7.0 * v[2]
        return v[0], -(back + v[0]), back - here, here + v[3], -v[3]

    def adjoint(levels, carry):
        moved = [
            (face_shifts(k, (-2, -1, 1)), [column_shifts(second, f, k, rim[4 + f]) for f in range(3)]) for k in levels
        ]
        for k, (uy, turned) in zip(levels, moved):
            for h in span:
                i = h * depth + k
                wets = wet_at(h, k)
                r = arms([first[at(2, h, k), top + s : end + s] for s in (-2, -1, 0, 1)], wets)
                c = arms([uy[-2][h], uy[-1][h], open_y[i], uy[1][h]], wets)
                weights = [(1.0 + r[2]) + c[2], r[0], r[1], r[3], r[4], c[0], c[1], c[3], c[4]]
                for f in range(3):
                    values = [second[at(f, h, k), top + s : end + s] for s in (0, -2, -1, 1, 2)]
                    values += [turned[f][s][h] for s in (-2, -1, 1, 2)]
                    terms = [w * m for w, m in zip(weights, values)]
                    if f == 2:
                        for n in range(9):
                            cross[at(n, h, k)] = terms[n]
                    else:
                        pairs = [terms[n] + terms[n + 1] for n in range(1, 9, 2)]
                        total = terms[0] + ((pairs[0] + pairs[1]) + (pairs[2] + pairs[3]))
                        (theta_adj, salt_adj)[f][i] = total
        return carry

    by_groups(0, depth, 5, adjoint, 0)
    for h in span:
        top_parts[h] = wet_at(h, 0) * second[at(0, h, 0), top:end]
        top_parts[halves + h] = 1.0 + 0.2 * (wet_at(h, 0) * second[at(2, h, 0), top:end])

    others(lambda i, device: sum_copy(i, device).wait_recv())
    sums[...] = jnp.broadcast_to(jnp.sum(slots[...], axis=0, keepdims=True), sums.shape)
    for copy, sends, _ in rims + stage_two:
        guarded(sends, copy.wait_send)
    others(lambda i, device: sum_copy(i, device).wait_send())


def finish_kernel(
    sizes,
    cross, theta_adj, salt_adj, k_fixed, k_zeta, basis, top_parts, sums,
    theta_out, salt_out, kappa_out, forcing_out,
    zeta, theta_grad, salt_grad, kappa_grad, forcing_grad, sems,
):
    depth, rows, cols = sizes
    halves = cols // LANES
    top, end = RIM, RIM + rows
    span = range(halves)
    lane = lane_index(rows)
    total = sums[...]
    for step in (8, 4, 2, 1):
        total = total + roll(total, -step)
    m = [jnp.broadcast_to(total[:, 16 * g : 16 * g + 1], (8, LANES)) for g in range(8)]
    m = m[:5] + [2.0 * m[5] - m[1], 2.0 * m[6] - m[0], 2.0 * m[7] - m[1]]
    weights = [jnp.concatenate([w] * ((rows + 2 * RIM) // 8), axis=0) for w in weights_from(m)]
    tiles = halves + 2
    for h in range(tiles):
        b = [basis[k * tiles + h] for k in range(ITERS)]
        zeta[h] = (weights[0] * b[0] + weights[1] * b[1]) + (weights[2] * b[2] + weights[3] * b[3])
    level = [zeta[h, top:end] for h in range(tiles)]
    around = []
    for h in span:
        near = [level[h + 1]] + [zeta[h + 1, top + s : end + s] for s in (-2, -1, 1, 2)]
        for s in (-2, -1, 1, 2):
            if s > 0:
                near.append(jnp.where(lane < LANES - s, roll(level[h + 1], -s), roll(level[h + 2], -s)))
            else:
                near.append(jnp.where(lane < -s, roll(level[h], -s), roll(level[h + 1], -s)))
        around.append(near)
    for h in span:
        forcing_grad[:, h * LANES : (h + 1) * LANES] = top_parts[h] + around[h][0] * top_parts[halves + h]
    put_forcing = pltpu.make_async_copy(forcing_grad, forcing_out, sems.at[0])
    put_forcing.start()
    group = 5
    groups = depth // group
    copies = [put_forcing]
    for g in range(groups + (depth % group > 0)):
        for k in range(g * group, min(depth, (g + 1) * group)):
            for h in span:
                i = h * depth + k
                where = slice(h * LANES, (h + 1) * LANES)
                terms = [cross[(n * halves + h) * depth + k] * around[h][n] for n in range(9)]
                pairs = [terms[n] + terms[n + 1] for n in range(1, 9, 2)]
                change = terms[0] + ((pairs[0] + pairs[1]) + (pairs[2] + pairs[3]))
                theta_grad[k, :, where] = theta_adj[i] + 0.2 * change
                salt_grad[k, :, where] = salt_adj[i] - 0.15 * change
                if k < depth - 1:
                    j = h * (depth - 1) + k
                    kappa_grad[k, :, where] = k_fixed[j] + k_zeta[j] * around[h][0]
        for src, dst in ((theta_grad, theta_out), (salt_grad, salt_out), (kappa_grad, kappa_out)):
            first, last = g * group, min(src.shape[0], (g + 1) * group)
            if first < last:
                part = pl.ds(first, last - first)
                copy = pltpu.make_async_copy(src.at[part], dst.at[part], sems.at[len(copies)])
                copy.start()
                copies.append(copy)
    for copy in copies:
        copy.wait()


def shards(*args):
    theta = args[0]
    depth, rows, cols = theta.shape
    halves = cols // LANES
    count = lax.axis_size("trow") * lax.axis_size("tcol")
    tall = rows + 2 * RIM
    V = pltpu.VMEM
    DMA = pltpu.SemaphoreType.DMA
    flat = V((halves * depth, rows, LANES), F32)
    ints = V((halves * depth, rows, LANES), jnp.int32)
    upper = V((halves * (depth - 1), rows, LANES), F32)
    tile = V((7, rows, LANES), F32)
    scratch = [
        flat, flat, flat, flat, ints, upper, V((rows, cols), F32), flat, flat,
        V((tall, cols + 2 * LANES), F32), V((tall, cols + 2 * LANES), jnp.int32),
        V((halves * depth, rows + RIM, LANES), F32), V((halves * depth, RIM, LANES), F32),
        V((3 * halves * depth, tall, LANES), F32), V((3 * halves * depth, tall, LANES), F32),
        flat, flat, flat, flat, flat, flat,
        tile, tile, tile, tile, V((count, LANES), F32),
        DMA((3 + 8 * halves,)), DMA((16,)), DMA((16,)), DMA((9,)), DMA((9,)), DMA((count,)), DMA((count,)),
    ]
    parts = [
        (9 * halves * depth, rows, LANES), (halves * depth, rows, LANES), (halves * depth, rows, LANES),
        (halves * (depth - 1), rows, LANES), (halves * (depth - 1), rows, LANES),
        (ITERS * (halves + 2), tall, LANES), (2 * halves, rows, LANES), (8, LANES),
    ]
    found = pl.pallas_call(
        functools.partial(solve_kernel, (depth, rows, cols)),
        out_shape=[jax.ShapeDtypeStruct(o, F32) for o in parts],
        in_specs=[pl.BlockSpec(memory_space=pltpu.HBM)] * len(args),
        out_specs=[pl.BlockSpec(memory_space=V)] * len(parts),
        scratch_shapes=scratch,
        compiler_params=pltpu.CompilerParams(
            collective_id=0, has_side_effects=True, vmem_limit_bytes=40 * 1024 * 1024
        ),
    )(*[pltpu.with_memory_space_constraint(a, pltpu.HBM) for a in args])
    outs = [(depth, rows, cols), (depth, rows, cols), (depth - 1, rows, cols), (rows, cols)]
    return tuple(
        pl.pallas_call(
            functools.partial(finish_kernel, (depth, rows, cols)),
            out_shape=[jax.ShapeDtypeStruct(o, F32) for o in outs],
            in_specs=[pl.BlockSpec(memory_space=V)] * len(parts),
            out_specs=[pl.BlockSpec(memory_space=pltpu.HBM)] * len(outs),
            scratch_shapes=[V((halves + 2, tall, LANES), F32)] + [V(o, F32) for o in outs] + [DMA((1 + 3 * (depth // 5 + 1),))],
            compiler_params=pltpu.CompilerParams(vmem_limit_bytes=16 * 1024 * 1024),
        )(*found)
    )


def solution(mesh):
    cube, plane = P(None, "trow", "tcol"), P("trow", "tcol")
    in_specs = (cube,) * 6 + (plane,) * 2 + (cube,) * 2 + (plane,)
    out_specs = (cube,) * 3 + (plane,)
    return jax.shard_map(shards, mesh=mesh, in_specs=in_specs, out_specs=out_specs, check_vma=False)
```

time: 35.4 us -> 23.7 us (0.67)
  the two profiles are of different devices: /device:TPU:0 before, /device:TPU:1 now
where the time goes in v2:
time: 23.7 us; the launch traced here: 23.6 us
  Pallas kernels  22.9 us (97%)
  between operations  0.64 us (3%)
    pallas_call x1, Pallas kernels, shards(): pl.pallas_call(functools.partial(solve_kernel, (depth, rows, cols)), out_...  21 us
    pallas_call x1, Pallas kernels, shards(): pl.pallas_call(functools.partial(finish_kernel, (depth, rows, cols)), out...  1.94 us

profile of v2, /device:TPU:1, one launch (start us, length us, event | category | flops | bytes accessed | tf_op | source)
XLA Modules:
  0.0 23.6 jit_solution(11450859044341255753)
XLA Ops:
  0.6 21.0 %shard_map.138 = (f32[450,16,128]{2,1,0:T(8,128)S(1)}, f32[50,16,128]{2,1,0:T(8,128)S(1)}, f32[50,16,128]{2,1,0:T(8,128)S(1)}, f32[48,16,128]{2,1,0:T(8,128)S(1)...) custom-call(f32[25,16,256]{2,1,0:T(8,128)} %theta_in.1, ...), custom_call_target="tpu_custom_call" | custom-call | tf_op jit(solution)/shard_map/pallas_call | solution.py:626
  21.6 1.9 %shard_map.139 = (f32[25,16,256]{2,1,0:T(8,128)}, f32[25,16,256]{2,1,0:T(8,128)}, f32[24,16,256]{2,1,0:T(8,128)}, f32[16,256]{1,0:T(8,128)}) custom-call(f32[450,16,128]{2,1,0:T(8,128)S(1)} %get-tuple-element.12.cross, f32[50,16,128]{2,1,0:T(8,128)S(1)} %get-tuple-element.13.theta_adj, f32[50,16,128]{2,1,0:T(8,128)S(1)} %get-tuple-element.14.salt_adj, ...), custom_call_target="tpu_custom_call" | custom-call | tf_op jit(solution)/shard_map/pallas_call | solution.py:638

commit v3 on v2

--- a/solution.py
+++ b/solution.py
@@ -88,14 +88,15 @@
     return pltpu.roll(x, amount % LANES if isinstance(amount, int) else amount & (LANES - 1), 1)
 
 
-def shifted(parts, rim, k, by, lane):
+def shifted(parts, ends, by, lane):
     if by > 0:
-        turned = [roll(p, -by) for p in parts] + [roll(rim, LANES - 4 * k - by)]
-        edge = LANES - by
+        joined = [jnp.where(lane < by, nearby, p) for p, nearby in zip(parts, parts[1:] + [ends])]
     else:
-        turned = [roll(rim, LANES - 4 * k - by)] + [roll(p, -by) for p in parts]
-        edge = -by
-    return [jnp.where(lane < edge, turned[h], turned[h + 1]) for h in range(len(parts))]
+        joined = [jnp.where(lane >= LANES + by, nearby, p) for p, nearby in zip(parts, [ends] + parts[:-1])]
+    return [roll(p, -by) for p in joined]
+
+
+GROUP = 5
 
 
 def by_groups(start, stop, group, body, carry):
@@ -103,6 +104,10 @@
     carry = lax.fori_loop(0, count, lambda i, c: body([start + i * group + u for u in range(group)], c), carry)
     rest = list(range(start + count * group, stop))
     return body(rest, carry) if rest else carry
+
+
+def signed_sum(terms):
+    return terms[0] + (((terms[1] + terms[2]) - (terms[5] + terms[6])) + ((terms[3] + terms[4]) - (terms[7] + terms[8])))
 
 
 def guarded(condition, action):
@@ -117,7 +122,7 @@
     cross, theta_adj, salt_adj, k_fixed, k_zeta, zeta, top_parts, sums,
     theta, salt, vx, vy, land, kappa, forcing, theta_cot, salt_cot,
     surface, bottom, wet, wet_after, first, second, open_y, inverse, link, ratio, theta_mix, salt_mix,
-    seam_own, seam_left, seam_right, rim, slots,
+    seam_own, seam_left, seam_right, ends, slots,
     local_sem, rim_send, rim_recv, halo_send, halo_recv, sum_send, sum_recv,
 ):
     depth, rows, cols = sizes
@@ -133,8 +138,11 @@
     blank = jnp.zeros((rows, LANES), F32)
     span = range(halves)
 
+    chunks = depth // GROUP
+    per_chunk = 3 * halves * GROUP
+
     def at(f, h, k):
-        return (f * halves + h) * depth + k
+        return (k * 3 + f) * halves + h
 
     surface[...] = jnp.zeros_like(surface)
     bottom[...] = jnp.zeros_like(bottom)
@@ -179,14 +187,54 @@
     get_salt = fetch_halves(salt_in, salt)
     get_vx = fetch_halves(vx_in, vx)
     get_vy = fetch_halves(vy_in, vy)
+    get_forcing = fetch(forcing_in, forcing)
     get_kappa = fetch_halves(kappa_in, kappa)
     get_theta_cot = fetch_halves(theta_cot_in, theta_cot)
     get_salt_cot = fetch_halves(salt_cot_in, salt_cot)
-    get_forcing = fetch(forcing_in, forcing)
 
     def arrived(copies):
         for copy in copies:
             copy.wait()
+
+    arrived([get_bottom] + get_land)
+
+    def wet_levels(levels, carry):
+        for k in levels:
+            for h in span:
+                depth_here = bottom[top:end, LANES * (h + 1) : LANES * (h + 2)]
+                wet[h * depth + k, 0:rows] = jnp.where(k < depth_here, land[h * depth + k].astype(F32), 0.0)
+                wet[h * depth + k, rows : rows + RIM] = jnp.ones((RIM, LANES), F32)
+        return carry
+
+    by_groups(0, depth, 5, wet_levels, 0)
+
+    def wet_at(h, k):
+        return wet[h * depth + k, 0:rows]
+
+    arrived(get_theta + get_salt + get_vx + get_vy)
+
+    def pack(k, parts, packed):
+        both = jnp.where(lane < LANES // 2, parts[0], parts[-1])
+        here = ((lane + 2 - 4 * k) & (LANES - 1)) < 4
+        return jnp.where(here, roll(both, 4 * k), packed)
+
+    def prepare(levels, packs):
+        for k in levels:
+            wets = [wet_at(h, k) for h in span]
+            qt, qs, uy = [], [], []
+            for h in span:
+                i = h * depth + k
+                qt.append(theta[i] * wets[h])
+                qs.append(salt[i] * wets[h])
+                uy.append(vy[i])
+                first[at(0, h, k), top:end] = qt[h]
+                first[at(1, h, k), top:end] = qs[h]
+                first[at(2, h, k), top:end] = vx[i] * wets[h] * wet[i, 1 : rows + 1] * (1.0 / 12.0)
+            packs = tuple(pack(k, parts, packed) for parts, packed in zip((qt, qs, uy, wets), packs))
+        return packs
+
+    for f, packed in enumerate(by_groups(0, depth, 5, prepare, (blank,) * 4)):
+        seam_own[f] = packed
 
     pl.semaphore_wait(barrier, count - 1)
 
@@ -215,46 +263,6 @@
     for copy, sends, _ in rims:
         guarded(sends, copy.start)
 
-    arrived([get_bottom] + get_land)
-
-    def wet_levels(levels, carry):
-        for k in levels:
-            for h in span:
-                depth_here = bottom[top:end, LANES * (h + 1) : LANES * (h + 2)]
-                wet[h * depth + k, 0:rows] = jnp.where(k < depth_here, land[h * depth + k].astype(F32), 0.0)
-                wet[h * depth + k, rows : rows + RIM] = jnp.ones((RIM, LANES), F32)
-        return carry
-
-    by_groups(0, depth, 5, wet_levels, 0)
-
-    def wet_at(h, k):
-        return wet[h * depth + k, 0:rows]
-
-    arrived(get_theta + get_salt + get_vx + get_vy)
-
-    def pack(k, parts, packed):
-        both = jnp.where(lane < LANES // 2, parts[0], parts[-1])
-        here = ((lane + 2 - 4 * k) & (LANES - 1)) < 4
-        return jnp.where(here, roll(both, 4 * k), packed)
-
-    def prepare(levels, packs):
-        for k in levels:
-            wets = [wet_at(h, k) for h in span]
-            qt, qs, uy = [], [], []
-            for h in span:
-                i = h * depth + k
-                qt.append(theta[i] * wets[h])
-                qs.append(salt[i] * wets[h])
-                uy.append(vy[i])
-                first[at(0, h, k), top:end] = qt[h]
-                first[at(1, h, k), top:end] = qs[h]
-                first[at(2, h, k), top:end] = vx[i] * wets[h] * wet[i, 1 : rows + 1] * (1.0 / 12.0)
-            packs = tuple(pack(k, parts, packed) for parts, packed in zip((qt, qs, uy, wets), packs))
-        return packs
-
-    for f, packed in enumerate(by_groups(0, depth, 5, prepare, (blank,) * 4)):
-        seam_own[f] = packed
-
     def remote(src, dst, i, device):
         return pltpu.make_async_remote_copy(
             src_ref=src, dst_ref=dst, send_sem=halo_send.at[i], recv_sem=halo_recv.at[i], device_id=device, device_id_type=MESH
@@ -262,16 +270,31 @@
 
     after, before = (row + 1, col), (row - 1, col)
     right, left = (row, col + 1), (row, col - 1)
-    low, high, below, above = pl.ds(end - 2, 2), pl.ds(top, 2), pl.ds(top - 2, 2), pl.ds(end, 2)
-    stage_one = [
-        (remote(first.at[:, low], first.at[:, below], 0, after), has_after, has_before),
-        (remote(first.at[:, high], first.at[:, above], 1, before), has_before, has_after),
-        (remote(wet.at[:, pl.ds(0, 1)], wet_after.at[:, pl.ds(0, 1)], 2, before), has_before, has_after),
-        (remote(seam_own.at[pl.ds(0, 4)], seam_left.at[pl.ds(0, 4)], 3, right), has_right, has_left),
-        (remote(seam_own.at[pl.ds(0, 4)], seam_right.at[pl.ds(0, 4)], 4, left), has_left, has_right),
-    ]
-    for copy, sends, _ in stage_one:
+    def row_copies(ref, base, g):
+        part = pl.ds(g * per_chunk, per_chunk)
+        return [
+            (remote(ref.at[part, pl.ds(end - 2, 2)], ref.at[part, pl.ds(top - 2, 2)], base + g, after), has_after, has_before),
+            (remote(ref.at[part, pl.ds(top, 2)], ref.at[part, pl.ds(end, 2)], base + chunks + g, before), has_before, has_after),
+        ]
+
+    def edge_copies(first_field, fields, base):
+        part = pl.ds(first_field, fields)
+        return [
+            (remote(seam_own.at[part], seam_left.at[part], base, right), has_right, has_left),
+            (remote(seam_own.at[part], seam_right.at[part], base + 1, left), has_left, has_right),
+        ]
+
+    def send_rows(ref, base):
+        for g in range(chunks):
+            for copy, sends, _ in row_copies(ref, base, g):
+                guarded(sends, copy.start)
+
+    edges_one, edges_two = edge_copies(0, 4, 0), edge_copies(4, 3, 2)
+    wet_copy = remote(wet.at[:, pl.ds(0, 1)], wet_after.at[:, pl.ds(0, 1)], 4, before)
+    rows_one, rows_two = 5, 5 + 2 * chunks
+    for copy, sends, _ in edges_one + [(wet_copy, has_before, has_after)]:
         guarded(sends, copy.start)
+    send_rows(first, rows_one)
 
     def clear(missing, ref, start):
         @pl.when(missing)
@@ -282,57 +305,6 @@
         clear(jnp.logical_not(has_before), ref, top - 2)
         clear(jnp.logical_not(has_after), ref, end)
     clear(jnp.logical_not(has_after), wet_after, 0)
-
-    get_surface.wait()
-    for copy, _, receives in rims:
-        guarded(receives, copy.wait_recv)
-    wide = (rows + 2 * RIM, cols + 2 * LANES)
-    row_at = lax.broadcasted_iota(jnp.int32, wide, 0) - RIM + row * rows
-    col_at = lax.broadcasted_iota(jnp.int32, wide, 1) - LANES + col * cols
-    inside = ((row_at >= 0) & (row_at < rows * mesh_rows)) & ((col_at >= 0) & (col_at < cols * mesh_cols))
-    scaled = (bottom[...].astype(F32) * (1.0 / depth) + (4.2 - CENTRE)) * (1.0 / RADIUS)
-    basis = [surface[...]]
-    for k in range(ITERS):
-        field = basis[-1]
-        beside = (pltpu.roll(field, 1, 0) + pltpu.roll(field, wide[0] - 1, 0)) + (
-            pltpu.roll(field, 1, 1) + pltpu.roll(field, wide[1] - 1, 1)
-        )
-        image = scaled * field - beside * (1.0 / RADIUS)
-        if k > 0:
-            image = 2.0 * image - basis[-2]
-        basis.append(jnp.where(inside, image, 0.0))
-
-    def own_product(a, b):
-        product = basis[a][top:end, LANES : LANES + cols] * basis[b][top:end, LANES : LANES + cols]
-        tiles = [product[i : i + 8, j : j + LANES] for i in range(0, rows, 8) for j in range(0, cols, LANES)]
-        return functools.reduce(jnp.add, tiles)
-
-    partial = [own_product(a, b) for a, b in ((0, 0), (0, 1), (0, 2), (0, 3), (0, 4), (2, 3), (3, 3), (3, 4))]
-    small_lane = lane_index(8)
-    width = LANES // 2
-    while len(partial) > 1:
-        half = len(partial) // 2
-        take_first = (small_lane & (2 * width - 1)) < width
-        partial = [
-            jnp.where(take_first, a + roll(a, -width), b + roll(b, width)) for a, b in zip(partial[:half], partial[half:])
-        ]
-        width //= 2
-    slots[0:1] = jnp.sum(partial[0], axis=0, keepdims=True)
-
-    def sum_copy(i, device):
-        return pltpu.make_async_remote_copy(
-            src_ref=slots.at[pl.ds(0, 1)],
-            dst_ref=slots.at[pl.ds(i, 1)],
-            send_sem=sum_send.at[i],
-            recv_sem=sum_recv.at[i],
-            device_id=device,
-            device_id_type=MESH,
-        )
-
-    others(lambda i, device: sum_copy(i, device).start())
-    for k in range(ITERS):
-        for h in range(halves + 2):
-            zeta[k * (halves + 2) + h] = basis[k][:, h * LANES : (h + 1) * LANES]
 
     arrived(get_kappa + get_theta_cot + get_salt_cot)
 
@@ -396,35 +368,88 @@
 
     for f, packed in enumerate(by_groups(0, depth, 5, pack_second, (blank,) * 3)):
         seam_own[4 + f] = packed
-    stage_two = [
-        (remote(second.at[:, low], second.at[:, below], 5, after), has_after, has_before),
-        (remote(second.at[:, high], second.at[:, above], 6, before), has_before, has_after),
-        (remote(seam_own.at[pl.ds(4, 3)], seam_left.at[pl.ds(4, 3)], 7, right), has_right, has_left),
-        (remote(seam_own.at[pl.ds(4, 3)], seam_right.at[pl.ds(4, 3)], 8, left), has_left, has_right),
-    ]
-    for copy, sends, _ in stage_two:
+    for copy, sends, _ in edges_two:
         guarded(sends, copy.start)
-
-    for copy, sends, receives in stage_one:
+    send_rows(second, rows_two)
+
+    get_surface.wait()
+    for copy, _, receives in rims:
+        guarded(receives, copy.wait_recv)
+    wide = (rows + 2 * RIM, cols + 2 * LANES)
+    row_at = lax.broadcasted_iota(jnp.int32, wide, 0) - RIM + row * rows
+    col_at = lax.broadcasted_iota(jnp.int32, wide, 1) - LANES + col * cols
+    inside = ((row_at >= 0) & (row_at < rows * mesh_rows)) & ((col_at >= 0) & (col_at < cols * mesh_cols))
+    scaled = (bottom[...].astype(F32) * (1.0 / depth) + (4.2 - CENTRE)) * (1.0 / RADIUS)
+    basis = [surface[...]]
+    for k in range(ITERS):
+        field = basis[-1]
+        beside = (pltpu.roll(field, 1, 0) + pltpu.roll(field, wide[0] - 1, 0)) + (
+            pltpu.roll(field, 1, 1) + pltpu.roll(field, wide[1] - 1, 1)
+        )
+        image = scaled * field - beside * (1.0 / RADIUS)
+        if k > 0:
+            image = 2.0 * image - basis[-2]
+        basis.append(jnp.where(inside, image, 0.0))
+
+    def own_product(a, b):
+        product = basis[a][top:end, LANES : LANES + cols] * basis[b][top:end, LANES : LANES + cols]
+        tiles = [product[i : i + 8, j : j + LANES] for i in range(0, rows, 8) for j in range(0, cols, LANES)]
+        return functools.reduce(jnp.add, tiles)
+
+    partial = [own_product(a, b) for a, b in ((0, 0), (0, 1), (0, 2), (0, 3), (0, 4), (2, 3), (3, 3), (3, 4))]
+    small_lane = lane_index(8)
+    width = LANES // 2
+    while len(partial) > 1:
+        half = len(partial) // 2
+        take_first = (small_lane & (2 * width - 1)) < width
+        partial = [
+            jnp.where(take_first, a + roll(a, -width), b + roll(b, width)) for a, b in zip(partial[:half], partial[half:])
+        ]
+        width //= 2
+    slots[0:1] = jnp.sum(partial[0], axis=0, keepdims=True)
+
+    def sum_copy(i, device):
+        return pltpu.make_async_remote_copy(
+            src_ref=slots.at[pl.ds(0, 1)],
+            dst_ref=slots.at[pl.ds(i, 1)],
+            send_sem=sum_send.at[i],
+            recv_sem=sum_recv.at[i],
+            device_id=device,
+            device_id_type=MESH,
+        )
+
+    others(lambda i, device: sum_copy(i, device).start())
+    for k in range(ITERS):
+        for h in range(halves + 2):
+            zeta[k * (halves + 2) + h] = basis[k][:, h * LANES : (h + 1) * LANES]
+
+    for copy, sends, receives in edges_one + [(wet_copy, has_before, has_after)]:
         guarded(sends, copy.wait_send)
         guarded(receives, copy.wait_recv)
-    faces = 2 * halves * depth
-    first[faces:, top - 1 : top] = first[faces:, top - 1 : top] * wet[:, 0:1]
-    first[faces:, end - 1 : end] = first[faces:, end - 1 : end] * wet_after[:, 0:1]
 
     def open_across(uy, near):
         return uy * near * roll(near, -1) * (1.0 / 12.0)
 
     inner_side = spot < 0
-    rim[0] = jnp.where(inner_side, seam_left[0], seam_right[0])
-    rim[1] = jnp.where(inner_side, seam_left[1], seam_right[1])
-    rim[3] = jnp.where(inner_side, seam_left[3], seam_right[3])
     open_left = open_across(seam_left[2], jnp.where(inner_side, seam_left[3], seam_own[3]))
     open_right = open_across(seam_right[2], seam_right[3])
-    rim[2] = jnp.where(inner_side, open_left, open_right)
+
+    def unpack(fields):
+        def one_group(levels, carry):
+            for k in levels:
+                for f, packed in fields:
+                    ends[f * depth + k] = roll(packed, LANES - 4 * k)
+            return carry
+
+        by_groups(0, depth, 5, one_group, 0)
+
+    def both_sides(f):
+        return jnp.where(inner_side, seam_left[f], seam_right[f])
+
+    unpack([(0, both_sides(0)), (1, both_sides(1)), (2, jnp.where(inner_side, open_left, open_right)), (3, both_sides(3))])
 
     def open_columns(levels, carry):
-        ahead = [shifted([wet_at(h, k) for h in span], rim[3], k, 1, lane) for k in levels]
+        ahead = [shifted([wet_at(h, k) for h in span], ends[3 * depth + k], 1, lane) for k in levels]
         for k, wets_ahead in zip(levels, ahead):
             for h in span:
                 i = h * depth + k
@@ -436,16 +461,28 @@
     for h in span:
         theta[h * depth] = theta[h * depth] + forcing[:, h * LANES : (h + 1) * LANES] * wet_at(h, 0)
 
-    def column_shifts(ref, f, k, edges):
+    def column_shifts(ref, f, k, beyond):
         centre = [ref[at(f, h, k), top:end] for h in span]
-        return {s: shifted(centre, edges, k, s, lane) for s in (-2, -1, 1, 2)}
+        return {s: shifted(centre, ends[beyond * depth + k], s, lane) for s in (-2, -1, 1, 2)}
 
     def face_shifts(k, steps):
         centre = [open_y[h * depth + k] for h in span]
-        return {s: shifted(centre, rim[2], k, s, lane) for s in steps}
+        return {s: shifted(centre, ends[2 * depth + k], s, lane) for s in steps}
+
+    def got_rows(ref, base, levels, sent_too):
+        for copy, sends, receives in row_copies(ref, base, lax.div(levels[0], GROUP)):
+            if sent_too:
+                guarded(sends, copy.wait_send)
+            guarded(receives, copy.wait_recv)
 
     def forward_down(levels, carry):
-        moved = [(face_shifts(k, (-1,)), [column_shifts(first, f, k, rim[f]) for f in range(2)]) for k in levels]
+        got_rows(first, rows_one, levels, True)
+        for k in levels:
+            for h in span:
+                f, i = at(2, h, k), h * depth + k
+                first[f, top - 1 : top] = first[f, top - 1 : top] * wet[i, 0:1]
+                first[f, end - 1 : end] = first[f, end - 1 : end] * wet_after[i, 0:1]
+        moved = [(face_shifts(k, (-1,)), [column_shifts(first, f, k, f) for f in range(2)]) for k in levels]
         for k, (uy, turned) in zip(levels, moved):
             out = []
             for h in span:
@@ -466,7 +503,7 @@
             carry = tuple(out)
         return carry
 
-    carry = by_groups(0, depth, 5, forward_down, ((blank, blank),) * halves)
+    carry = by_groups(0, depth, GROUP, forward_down, ((blank, blank),) * halves)
 
     def forward_up(steps, carry):
         for n in steps:
@@ -489,19 +526,20 @@
 
     by_groups(0, depth - 1, 4, forward_up, carry)
 
-    for copy, _, receives in stage_two:
+    for copy, sends, receives in edges_two:
+        guarded(sends, copy.wait_send)
         guarded(receives, copy.wait_recv)
-    for f in range(3):
-        rim[4 + f] = jnp.where(inner_side, seam_left[4 + f], seam_right[4 + f])
+    unpack([(4 + f, both_sides(4 + f)) for f in range(3)])
 
     def arms(u, wets):
         v = [wets * x for x in u]
         back, here = 7.0 * v[1], 7.0 * v[2]
-        return v[0], -(back + v[0]), back - here, here + v[3], -v[3]
+        return v[0], back + v[0], back - here, here + v[3], v[3]
 
     def adjoint(levels, carry):
+        got_rows(second, rows_two, levels, True)
         moved = [
-            (face_shifts(k, (-2, -1, 1)), [column_shifts(second, f, k, rim[4 + f]) for f in range(3)]) for k in levels
+            (face_shifts(k, (-2, -1, 1)), [column_shifts(second, f, k, 4 + f) for f in range(3)]) for k in levels
         ]
         for k, (uy, turned) in zip(levels, moved):
             for h in span:
@@ -509,28 +547,28 @@
                 wets = wet_at(h, k)
                 r = arms([first[at(2, h, k), top + s : end + s] for s in (-2, -1, 0, 1)], wets)
                 c = arms([uy[-2][h], uy[-1][h], open_y[i], uy[1][h]], wets)
-                weights = [(1.0 + r[2]) + c[2], r[0], r[1], r[3], r[4], c[0], c[1], c[3], c[4]]
+                weights = [(1.0 + r[2]) + c[2], r[0], r[3], c[0], c[3], r[1], r[4], c[1], c[4]]
                 for f in range(3):
-                    values = [second[at(f, h, k), top + s : end + s] for s in (0, -2, -1, 1, 2)]
-                    values += [turned[f][s][h] for s in (-2, -1, 1, 2)]
+                    values = [second[at(f, h, k), top + s : end + s] for s in (0, -2, 1)]
+                    values += [turned[f][s][h] for s in (-2, 1)]
+                    values += [second[at(f, h, k), top + s : end + s] for s in (-1, 2)]
+                    values += [turned[f][s][h] for s in (-1, 2)]
                     terms = [w * m for w, m in zip(weights, values)]
                     if f == 2:
                         for n in range(9):
-                            cross[at(n, h, k)] = terms[n]
+                            cross[(n * halves + h) * depth + k] = terms[n]
                     else:
-                        pairs = [terms[n] + terms[n + 1] for n in range(1, 9, 2)]
-                        total = terms[0] + ((pairs[0] + pairs[1]) + (pairs[2] + pairs[3]))
-                        (theta_adj, salt_adj)[f][i] = total
+                        (theta_adj, salt_adj)[f][i] = signed_sum(terms)
         return carry
 
-    by_groups(0, depth, 5, adjoint, 0)
+    by_groups(0, depth, GROUP, adjoint, 0)
     for h in span:
         top_parts[h] = wet_at(h, 0) * second[at(0, h, 0), top:end]
         top_parts[halves + h] = 1.0 + 0.2 * (wet_at(h, 0) * second[at(2, h, 0), top:end])
 
     others(lambda i, device: sum_copy(i, device).wait_recv())
     sums[...] = jnp.broadcast_to(jnp.sum(slots[...], axis=0, keepdims=True), sums.shape)
-    for copy, sends, _ in rims + stage_two:
+    for copy, sends, _ in rims:
         guarded(sends, copy.wait_send)
     others(lambda i, device: sum_copy(i, device).wait_send())
 
@@ -559,13 +597,16 @@
     level = [zeta[h, top:end] for h in range(tiles)]
     around = []
     for h in span:
-        near = [level[h + 1]] + [zeta[h + 1, top + s : end + s] for s in (-2, -1, 1, 2)]
-        for s in (-2, -1, 1, 2):
-            if s > 0:
-                near.append(jnp.where(lane < LANES - s, roll(level[h + 1], -s), roll(level[h + 2], -s)))
-            else:
-                near.append(jnp.where(lane < -s, roll(level[h], -s), roll(level[h + 1], -s)))
-        around.append(near)
+        by_row = {s: zeta[h + 1, top + s : end + s] for s in (-2, -1, 1, 2)}
+        by_col = {
+            s: jnp.where(lane < LANES - s, roll(level[h + 1], -s), roll(level[h + 2], -s))
+            if s > 0
+            else jnp.where(lane < -s, roll(level[h], -s), roll(level[h + 1], -s))
+            for s in (-2, -1, 1, 2)
+        }
+        around.append(
+            [level[h + 1], by_row[-2], by_row[1], by_col[-2], by_col[1], by_row[-1], by_row[2], by_col[-1], by_col[2]]
+        )
     for h in span:
         forcing_grad[:, h * LANES : (h + 1) * LANES] = top_parts[h] + around[h][0] * top_parts[halves + h]
     put_forcing = pltpu.make_async_copy(forcing_grad, forcing_out, sems.at[0])
@@ -579,8 +620,7 @@
                 i = h * depth + k
                 where = slice(h * LANES, (h + 1) * LANES)
                 terms = [cross[(n * halves + h) * depth + k] * around[h][n] for n in range(9)]
-                pairs = [terms[n] + terms[n + 1] for n in range(1, 9, 2)]
-                change = terms[0] + ((pairs[0] + pairs[1]) + (pairs[2] + pairs[3]))
+                change = signed_sum(terms)
                 theta_grad[k, :, where] = theta_adj[i] + 0.2 * change
                 salt_grad[k, :, where] = salt_adj[i] - 0.15 * change
                 if k < depth - 1:
@@ -609,14 +649,15 @@
     ints = V((halves * depth, rows, LANES), jnp.int32)
     upper = V((halves * (depth - 1), rows, LANES), F32)
     tile = V((7, rows, LANES), F32)
+    halo = DMA((5 + 4 * (depth // GROUP),))
     scratch = [
         flat, flat, flat, flat, ints, upper, V((rows, cols), F32), flat, flat,
         V((tall, cols + 2 * LANES), F32), V((tall, cols + 2 * LANES), jnp.int32),
         V((halves * depth, rows + RIM, LANES), F32), V((halves * depth, RIM, LANES), F32),
         V((3 * halves * depth, tall, LANES), F32), V((3 * halves * depth, tall, LANES), F32),
         flat, flat, flat, flat, flat, flat,
-        tile, tile, tile, tile, V((count, LANES), F32),
-        DMA((3 + 8 * halves,)), DMA((16,)), DMA((16,)), DMA((9,)), DMA((9,)), DMA((count,)), DMA((count,)),
+        tile, tile, tile, V((7 * depth, rows, LANES), F32), V((count, LANES), F32),
+        DMA((3 + 8 * halves,)), DMA((16,)), DMA((16,)), halo, halo, DMA((count,)), DMA((count,)),
     ]
     parts = [
         (9 * halves * depth, rows, LANES), (halves * depth, rows, LANES), (halves * depth, rows, LANES),

time: 23.7 us -> 21.1 us (0.89)
  the two profiles are of different devices: /device:TPU:1 before, /device:TPU:0 now
where the time goes in v3:
time: 21.1 us; the launch traced here: 20.8 us
  Pallas kernels  20.1 us (95%)
  between operations  0.64 us (3%)
    pallas_call x1, Pallas kernels, shards(): pl.pallas_call(functools.partial(solve_kernel, (depth, rows, cols)), out_...  18.2 us
    pallas_call x1, Pallas kernels, shards(): pl.pallas_call(functools.partial(finish_kernel, (depth, rows, cols)), out...  1.97 us

profile of v3, /device:TPU:0, one launch (start us, length us, event | category | flops | bytes accessed | tf_op | source)
XLA Modules:
  0.0 20.8 jit_solution(5731446453170688023)
XLA Ops:
  0.6 18.2 %shard_map.138 = (f32[450,16,128]{2,1,0:T(8,128)S(1)}, f32[50,16,128]{2,1,0:T(8,128)S(1)}, f32[50,16,128]{2,1,0:T(8,128)S(1)}, f32[48,16,128]{2,1,0:T(8,128)S(1)...) custom-call(f32[25,16,256]{2,1,0:T(8,128)} %theta_in.1, ...), custom_call_target="tpu_custom_call" | custom-call | tf_op jit(solution)/shard_map/pallas_call | solution.py:667
  18.8 2.0 %shard_map.139 = (f32[25,16,256]{2,1,0:T(8,128)}, f32[25,16,256]{2,1,0:T(8,128)}, f32[24,16,256]{2,1,0:T(8,128)}, f32[16,256]{1,0:T(8,128)}) custom-call(f32[450,16,128]{2,1,0:T(8,128)S(1)} %get-tuple-element.12.cross, f32[50,16,128]{2,1,0:T(8,128)S(1)} %get-tuple-element.13.theta_adj, f32[50,16,128]{2,1,0:T(8,128)S(1)} %get-tuple-element.14.salt_adj, ...), custom_call_target="tpu_custom_call" | custom-call | tf_op jit(solution)/shard_map/pallas_call | solution.py:679

commit v4 on v3

--- a/solution.py
+++ b/solution.py
@@ -119,10 +119,10 @@
 def solve_kernel(
     sizes,
     theta_in, salt_in, vx_in, vy_in, land_in, kappa_in, forcing_in, bottom_in, theta_cot_in, salt_cot_in, surface_in,
-    cross, theta_adj, salt_adj, k_fixed, k_zeta, zeta, top_parts, sums,
+    theta_grad, salt_grad, kappa_grad, forcing_grad,
     theta, salt, vx, vy, land, kappa, forcing, theta_cot, salt_cot,
     surface, bottom, wet, wet_after, first, second, open_y, inverse, link, ratio, theta_mix, salt_mix,
-    seam_own, seam_left, seam_right, ends, slots,
+    seam_own, seam_left, seam_right, ends, slots, cross, k_fixed, k_zeta, zeta,
     local_sem, rim_send, rim_recv, halo_send, halo_recv, sum_send, sum_recv,
 ):
     depth, rows, cols = sizes
@@ -526,113 +526,98 @@
 
     by_groups(0, depth - 1, 4, forward_up, carry)
 
-    for copy, sends, receives in edges_two:
-        guarded(sends, copy.wait_send)
-        guarded(receives, copy.wait_recv)
-    unpack([(4 + f, both_sides(4 + f)) for f in range(3)])
-
     def arms(u, wets):
         v = [wets * x for x in u]
         back, here = 7.0 * v[1], 7.0 * v[2]
         return v[0], back + v[0], back - here, here + v[3], v[3]
 
-    def adjoint(levels, carry):
-        got_rows(second, rows_two, levels, True)
-        moved = [
-            (face_shifts(k, (-2, -1, 1)), [column_shifts(second, f, k, 4 + f) for f in range(3)]) for k in levels
-        ]
-        for k, (uy, turned) in zip(levels, moved):
+    def coefficients(levels, carry):
+        moved = [face_shifts(k, (-2, -1, 1)) for k in levels]
+        for k, uy in zip(levels, moved):
             for h in span:
                 i = h * depth + k
                 wets = wet_at(h, k)
                 r = arms([first[at(2, h, k), top + s : end + s] for s in (-2, -1, 0, 1)], wets)
                 c = arms([uy[-2][h], uy[-1][h], open_y[i], uy[1][h]], wets)
-                weights = [(1.0 + r[2]) + c[2], r[0], r[3], c[0], c[3], r[1], r[4], c[1], c[4]]
-                for f in range(3):
+                for n, w in enumerate([(1.0 + r[2]) + c[2], r[0], r[3], c[0], c[3], r[1], r[4], c[1], c[4]]):
+                    cross[9 * i + n] = w
+        return carry
+
+    by_groups(0, depth, GROUP, coefficients, 0)
+
+    others(lambda i, device: sum_copy(i, device).wait_recv())
+    total = jnp.broadcast_to(jnp.sum(slots[...], axis=0, keepdims=True), (8, LANES))
+    for step in (8, 4, 2, 1):
+        total = total + roll(total, -step)
+    m = [jnp.broadcast_to(total[:, 16 * g : 16 * g + 1], (8, LANES)) for g in range(8)]
+    m = m[:5] + [2.0 * m[5] - m[1], 2.0 * m[6] - m[0], 2.0 * m[7] - m[1]]
+    weights = [jnp.concatenate([w] * (wide[0] // 8), axis=0) for w in weights_from(m)]
+    tiles = halves + 2
+    for h in range(tiles):
+        b = [zeta[k * tiles + h] for k in range(ITERS)]
+        zeta[h] = (weights[0] * b[0] + weights[1] * b[1]) + (weights[2] * b[2] + weights[3] * b[3])
+
+    for copy, sends, receives in edges_two:
+        guarded(sends, copy.wait_send)
+        guarded(receives, copy.wait_recv)
+    beyond = jnp.where(lane >= LANES // 2, zeta[0, top:end], zeta[tiles - 1, top:end])
+    far_t, far_s, far_w = both_sides(4), both_sides(5), both_sides(6)
+
+    def unpack_mu(levels, carry):
+        for k in levels:
+            turned = [roll(p, LANES - 4 * k) for p in (far_t, far_s, far_w)]
+            lifted = turned[2] * beyond
+            ends[4 * depth + k] = turned[0] + 0.2 * lifted
+            ends[5 * depth + k] = turned[1] - 0.15 * lifted
+        return carry
+
+    by_groups(0, depth, 5, unpack_mu, 0)
+
+    def finish(levels, carry):
+        got_rows(second, rows_two, levels, True)
+        for k in levels:
+            for h in span:
+                area = pl.ds(top - 2, rows + 8)
+                lifted = second[at(2, h, k), area] * zeta[h + 1, area]
+                second[at(0, h, k), area] = second[at(0, h, k), area] + 0.2 * lifted
+                second[at(1, h, k), area] = second[at(1, h, k), area] - 0.15 * lifted
+        moved = [[column_shifts(second, f, k, 4 + f) for f in range(2)] for k in levels]
+        for k, turned in zip(levels, moved):
+            for h in span:
+                i = h * depth + k
+                where = slice(h * LANES, (h + 1) * LANES)
+                for f, out in ((0, theta_grad), (1, salt_grad)):
                     values = [second[at(f, h, k), top + s : end + s] for s in (0, -2, 1)]
                     values += [turned[f][s][h] for s in (-2, 1)]
                     values += [second[at(f, h, k), top + s : end + s] for s in (-1, 2)]
                     values += [turned[f][s][h] for s in (-1, 2)]
-                    terms = [w * m for w, m in zip(weights, values)]
-                    if f == 2:
-                        for n in range(9):
-                            cross[(n * halves + h) * depth + k] = terms[n]
-                    else:
-                        (theta_adj, salt_adj)[f][i] = signed_sum(terms)
-        return carry
-
-    by_groups(0, depth, GROUP, adjoint, 0)
+                    out[k, :, where] = signed_sum([cross[9 * i + n] * v for n, v in enumerate(values)])
+        return carry
+
+    by_groups(0, depth, GROUP, finish, 0)
+
+    def finish_kappa(levels, carry):
+        for k in levels:
+            for h in span:
+                j = h * (depth - 1) + k
+                kappa_grad[k, :, h * LANES : (h + 1) * LANES] = k_fixed[j] + k_zeta[j] * zeta[h + 1, top:end]
+        return carry
+
+    by_groups(0, depth - 1, 4, finish_kappa, 0)
     for h in span:
-        top_parts[h] = wet_at(h, 0) * second[at(0, h, 0), top:end]
-        top_parts[halves + h] = 1.0 + 0.2 * (wet_at(h, 0) * second[at(2, h, 0), top:end])
-
-    others(lambda i, device: sum_copy(i, device).wait_recv())
-    sums[...] = jnp.broadcast_to(jnp.sum(slots[...], axis=0, keepdims=True), sums.shape)
+        forcing_grad[:, h * LANES : (h + 1) * LANES] = zeta[h + 1, top:end] + wet_at(h, 0) * second[at(0, h, 0), top:end]
+
     for copy, sends, _ in rims:
         guarded(sends, copy.wait_send)
     others(lambda i, device: sum_copy(i, device).wait_send())
 
 
-def finish_kernel(
-    sizes,
-    cross, theta_adj, salt_adj, k_fixed, k_zeta, basis, top_parts, sums,
-    theta_out, salt_out, kappa_out, forcing_out,
-    zeta, theta_grad, salt_grad, kappa_grad, forcing_grad, sems,
-):
-    depth, rows, cols = sizes
-    halves = cols // LANES
-    top, end = RIM, RIM + rows
-    span = range(halves)
-    lane = lane_index(rows)
-    total = sums[...]
-    for step in (8, 4, 2, 1):
-        total = total + roll(total, -step)
-    m = [jnp.broadcast_to(total[:, 16 * g : 16 * g + 1], (8, LANES)) for g in range(8)]
-    m = m[:5] + [2.0 * m[5] - m[1], 2.0 * m[6] - m[0], 2.0 * m[7] - m[1]]
-    weights = [jnp.concatenate([w] * ((rows + 2 * RIM) // 8), axis=0) for w in weights_from(m)]
-    tiles = halves + 2
-    for h in range(tiles):
-        b = [basis[k * tiles + h] for k in range(ITERS)]
-        zeta[h] = (weights[0] * b[0] + weights[1] * b[1]) + (weights[2] * b[2] + weights[3] * b[3])
-    level = [zeta[h, top:end] for h in range(tiles)]
-    around = []
-    for h in span:
-        by_row = {s: zeta[h + 1, top + s : end + s] for s in (-2, -1, 1, 2)}
-        by_col = {
-            s: jnp.where(lane < LANES - s, roll(level[h + 1], -s), roll(level[h + 2], -s))
-            if s > 0
-            else jnp.where(lane < -s, roll(level[h], -s), roll(level[h + 1], -s))
-            for s in (-2, -1, 1, 2)
-        }
-        around.append(
-            [level[h + 1], by_row[-2], by_row[1], by_col[-2], by_col[1], by_row[-1], by_row[2], by_col[-1], by_col[2]]
-        )
-    for h in span:
-        forcing_grad[:, h * LANES : (h + 1) * LANES] = top_parts[h] + around[h][0] * top_parts[halves + h]
-    put_forcing = pltpu.make_async_copy(forcing_grad, forcing_out, sems.at[0])
-    put_forcing.start()
-    group = 5
-    groups = depth // group
-    copies = [put_forcing]
-    for g in range(groups + (depth % group > 0)):
-        for k in range(g * group, min(depth, (g + 1) * group)):
-            for h in span:
-                i = h * depth + k
-                where = slice(h * LANES, (h + 1) * LANES)
-                terms = [cross[(n * halves + h) * depth + k] * around[h][n] for n in range(9)]
-                change = signed_sum(terms)
-                theta_grad[k, :, where] = theta_adj[i] + 0.2 * change
-                salt_grad[k, :, where] = salt_adj[i] - 0.15 * change
-                if k < depth - 1:
-                    j = h * (depth - 1) + k
-                    kappa_grad[k, :, where] = k_fixed[j] + k_zeta[j] * around[h][0]
-        for src, dst in ((theta_grad, theta_out), (salt_grad, salt_out), (kappa_grad, kappa_out)):
-            first, last = g * group, min(src.shape[0], (g + 1) * group)
-            if first < last:
-                part = pl.ds(first, last - first)
-                copy = pltpu.make_async_copy(src.at[part], dst.at[part], sems.at[len(copies)])
-                copy.start()
-                copies.append(copy)
+def write_kernel(*refs):
+    count = (len(refs) - 1) // 2
+    sems = refs[-1]
+    copies = [pltpu.make_async_copy(refs[i], refs[count + i], sems.at[i]) for i in range(count)]
+    for copy in copies:
+        copy.start()
     for copy in copies:
         copy.wait()
 
@@ -657,32 +642,29 @@
         V((3 * halves * depth, tall, LANES), F32), V((3 * halves * depth, tall, LANES), F32),
         flat, flat, flat, flat, flat, flat,
         tile, tile, tile, V((7 * depth, rows, LANES), F32), V((count, LANES), F32),
+        V((9 * halves * depth, rows, LANES), F32), upper, upper, V((ITERS * (halves + 2), tall, LANES), F32),
         DMA((3 + 8 * halves,)), DMA((16,)), DMA((16,)), halo, halo, DMA((count,)), DMA((count,)),
     ]
-    parts = [
-        (9 * halves * depth, rows, LANES), (halves * depth, rows, LANES), (halves * depth, rows, LANES),
-        (halves * (depth - 1), rows, LANES), (halves * (depth - 1), rows, LANES),
-        (ITERS * (halves + 2), tall, LANES), (2 * halves, rows, LANES), (8, LANES),
-    ]
+    outs = [(depth, rows, cols), (depth, rows, cols), (depth - 1, rows, cols), (rows, cols)]
+    shapes = [jax.ShapeDtypeStruct(o, F32) for o in outs]
     found = pl.pallas_call(
         functools.partial(solve_kernel, (depth, rows, cols)),
-        out_shape=[jax.ShapeDtypeStruct(o, F32) for o in parts],
+        out_shape=shapes,
         in_specs=[pl.BlockSpec(memory_space=pltpu.HBM)] * len(args),
-        out_specs=[pl.BlockSpec(memory_space=V)] * len(parts),
+        out_specs=[pl.BlockSpec(memory_space=V)] * len(outs),
         scratch_shapes=scratch,
         compiler_params=pltpu.CompilerParams(
             collective_id=0, has_side_effects=True, vmem_limit_bytes=40 * 1024 * 1024
         ),
     )(*[pltpu.with_memory_space_constraint(a, pltpu.HBM) for a in args])
-    outs = [(depth, rows, cols), (depth, rows, cols), (depth - 1, rows, cols), (rows, cols)]
     return tuple(
         pl.pallas_call(
-            functools.partial(finish_kernel, (depth, rows, cols)),
-            out_shape=[jax.ShapeDtypeStruct(o, F32) for o in outs],
-            in_specs=[pl.BlockSpec(memory_space=V)] * len(parts),
+            write_kernel,
+            out_shape=shapes,
+            in_specs=[pl.BlockSpec(memory_space=V)] * len(outs),
             out_specs=[pl.BlockSpec(memory_space=pltpu.HBM)] * len(outs),
-            scratch_shapes=[V((halves + 2, tall, LANES), F32)] + [V(o, F32) for o in outs] + [DMA((1 + 3 * (depth // 5 + 1),))],
-            compiler_params=pltpu.CompilerParams(vmem_limit_bytes=16 * 1024 * 1024),
+            scratch_shapes=[DMA((len(outs),))],
+            compiler_params=pltpu.CompilerParams(vmem_limit_bytes=1024 * 1024),
         )(*found)
     )
 

time: 21.1 us -> 22.4 us (1.062)
  Pallas kernels: 20.1 us -> 21.6 us
    pallas_call x1, Pallas kernels: 18.2 us -> 20.5 us  [shards(): pl.pallas_call(functools.partial(solve_kernel, (depth, rows, cols)), out_...]
    pallas_call x1, Pallas kernels: 1.97 us -> 1.06 us  [shards(): pl.pallas_call(write_kernel, out_shape=shapes, in_specs=[pl.BlockSpec(mem...]
where the time goes in v4:
time: 22.4 us; the launch traced here: 22.2 us
  Pallas kernels  21.6 us (96%)
  between operations  0.64 us (3%)
    pallas_call x1, Pallas kernels, shards(): pl.pallas_call(functools.partial(solve_kernel, (depth, rows, cols)), out_...  20.5 us
    pallas_call x1, Pallas kernels, shards(): pl.pallas_call(write_kernel, out_shape=shapes, in_specs=[pl.BlockSpec(mem...  1.06 us

profile of v4, /device:TPU:0, one launch (start us, length us, event | category | flops | bytes accessed | tf_op | source)
XLA Modules:
  0.0 22.2 jit_solution(16982909477390134109)
XLA Ops:
  0.6 20.5 %shard_map.138 = (f32[25,16,256]{2,1,0:T(8,128)S(1)}, f32[25,16,256]{2,1,0:T(8,128)S(1)}, f32[24,16,256]{2,1,0:T(8,128)S(1)}, f32[16,256]{1,0:T(8,128)S(1)}) custom-call(f32[25,16,256]{2,1,0:T(8,128)} %theta_in.1, f32[25,16,256]{2,1,0:T(8,128)} %salt_in.1, f32[25,16,256]{2,1,0:T(8,128)} %vx_in.1, f32[25,16,256]{2,1,0:T(8,128)} %vy_in.1, ...), custom_call_target="tpu_custom_call" | custom-call | tf_op jit(solution)/shard_map/pallas_call | solution.py:650
  21.2 1.1 %shard_map.139 = (f32[25,16,256]{2,1,0:T(8,128)}, f32[25,16,256]{2,1,0:T(8,128)}, f32[24,16,256]{2,1,0:T(8,128)}, f32[16,256]{1,0:T(8,128)}) custom-call(f32[25,16,256]{2,1,0:T(8,128)S(1)} %get-tuple-element.8.refs_0_, f32[25,16,256]{2,1,0:T(8,128)S(1)} %get-tuple-element.9.refs_1_, f32[24,16,256]{2,1,0:T(8,128)S(1)} %get-tuple-element.10.refs_2_, ...), custom_call_target="tpu_custom_call" | custom-call | tf_op jit(solution)/shard_map/pallas_call | solution.py:661

commit v5 on v4

--- a/solution.py
+++ b/solution.py
@@ -368,10 +368,6 @@
 
     for f, packed in enumerate(by_groups(0, depth, 5, pack_second, (blank,) * 3)):
         seam_own[4 + f] = packed
-    for copy, sends, _ in edges_two:
-        guarded(sends, copy.start)
-    send_rows(second, rows_two)
-
     get_surface.wait()
     for copy, _, receives in rims:
         guarded(receives, copy.wait_recv)
@@ -422,6 +418,10 @@
     for k in range(ITERS):
         for h in range(halves + 2):
             zeta[k * (halves + 2) + h] = basis[k][:, h * LANES : (h + 1) * LANES]
+
+    for copy, sends, _ in edges_two:
+        guarded(sends, copy.start)
+    send_rows(second, rows_two)
 
     for copy, sends, receives in edges_one + [(wet_copy, has_before, has_after)]:
         guarded(sends, copy.wait_send)

time: 22.4 us -> 20.2 us (0.902)
  Pallas kernels: 21.6 us -> 19.4 us
    pallas_call x1, Pallas kernels: 20.5 us -> 18.4 us  [shards(): pl.pallas_call(functools.partial(solve_kernel, (depth, rows, cols)), out_...]
where the time goes in v5:
time: 20.2 us; the launch traced here: 20 us
  Pallas kernels  19.4 us (96%)
  between operations  0.64 us (3%)
    pallas_call x1, Pallas kernels, shards(): pl.pallas_call(functools.partial(solve_kernel, (depth, rows, cols)), out_...  18.4 us
    pallas_call x1, Pallas kernels, shards(): pl.pallas_call(write_kernel, out_shape=shapes, in_specs=[pl.BlockSpec(mem...  1.06 us

profile of v5, /device:TPU:0, one launch (start us, length us, event | category | flops | bytes accessed | tf_op | source)
XLA Modules:
  0.0 20.0 jit_solution(7133507211212097157)
XLA Ops:
  0.6 18.4 %shard_map.138 = (f32[25,16,256]{2,1,0:T(8,128)S(1)}, f32[25,16,256]{2,1,0:T(8,128)S(1)}, f32[24,16,256]{2,1,0:T(8,128)S(1)}, f32[16,256]{1,0:T(8,128)S(1)}) custom-call(f32[25,16,256]{2,1,0:T(8,128)} %theta_in.1, f32[25,16,256]{2,1,0:T(8,128)} %salt_in.1, f32[25,16,256]{2,1,0:T(8,128)} %vx_in.1, f32[25,16,256]{2,1,0:T(8,128)} %vy_in.1, ...), custom_call_target="tpu_custom_call" | custom-call | tf_op jit(solution)/shard_map/pallas_call | solution.py:650
  19.0 1.1 %shard_map.139 = (f32[25,16,256]{2,1,0:T(8,128)}, f32[25,16,256]{2,1,0:T(8,128)}, f32[24,16,256]{2,1,0:T(8,128)}, f32[16,256]{1,0:T(8,128)}) custom-call(f32[25,16,256]{2,1,0:T(8,128)S(1)} %get-tuple-element.8.refs_0_, f32[25,16,256]{2,1,0:T(8,128)S(1)} %get-tuple-element.9.refs_1_, f32[24,16,256]{2,1,0:T(8,128)S(1)} %get-tuple-element.10.refs_2_, ...), custom_call_target="tpu_custom_call" | custom-call | tf_op jit(solution)/shard_map/pallas_call | solution.py:661

commit v6 on v5

--- a/solution.py
+++ b/solution.py
@@ -121,7 +121,7 @@
     theta_in, salt_in, vx_in, vy_in, land_in, kappa_in, forcing_in, bottom_in, theta_cot_in, salt_cot_in, surface_in,
     theta_grad, salt_grad, kappa_grad, forcing_grad,
     theta, salt, vx, vy, land, kappa, forcing, theta_cot, salt_cot,
-    surface, bottom, wet, wet_after, first, second, open_y, inverse, link, ratio, theta_mix, salt_mix,
+    surface, bottom, wet, wet_after, face_x, first, second, open_y, inverse, link, ratio, theta_mix, salt_mix,
     seam_own, seam_left, seam_right, ends, slots, cross, k_fixed, k_zeta, zeta,
     local_sem, rim_send, rim_recv, halo_send, halo_recv, sum_send, sum_recv,
 ):
@@ -139,10 +139,12 @@
     span = range(halves)
 
     chunks = depth // GROUP
-    per_chunk = 3 * halves * GROUP
 
     def at(f, h, k):
         return (k * 3 + f) * halves + h
+
+    def at_first(f, h, k):
+        return (k * 2 + f) * halves + h
 
     surface[...] = jnp.zeros_like(surface)
     bottom[...] = jnp.zeros_like(bottom)
@@ -227,9 +229,9 @@
                 qt.append(theta[i] * wets[h])
                 qs.append(salt[i] * wets[h])
                 uy.append(vy[i])
-                first[at(0, h, k), top:end] = qt[h]
-                first[at(1, h, k), top:end] = qs[h]
-                first[at(2, h, k), top:end] = vx[i] * wets[h] * wet[i, 1 : rows + 1] * (1.0 / 12.0)
+                first[at_first(0, h, k), top:end] = qt[h]
+                first[at_first(1, h, k), top:end] = qs[h]
+                face_x[i, top:end] = vx[i] * wets[h] * wet[i, 1 : rows + 1] * (1.0 / 12.0)
             packs = tuple(pack(k, parts, packed) for parts, packed in zip((qt, qs, uy, wets), packs))
         return packs
 
@@ -271,6 +273,7 @@
     after, before = (row + 1, col), (row - 1, col)
     right, left = (row, col + 1), (row, col - 1)
     def row_copies(ref, base, g):
+        per_chunk = ref.shape[0] // chunks
         part = pl.ds(g * per_chunk, per_chunk)
         return [
             (remote(ref.at[part, pl.ds(end - 2, 2)], ref.at[part, pl.ds(top - 2, 2)], base + g, after), has_after, has_before),
@@ -291,8 +294,11 @@
 
     edges_one, edges_two = edge_copies(0, 4, 0), edge_copies(4, 3, 2)
     wet_copy = remote(wet.at[:, pl.ds(0, 1)], wet_after.at[:, pl.ds(0, 1)], 4, before)
-    rows_one, rows_two = 5, 5 + 2 * chunks
-    for copy, sends, _ in edges_one + [(wet_copy, has_before, has_after)]:
+    faces_down = remote(face_x.at[:, pl.ds(end - 2, 2)], face_x.at[:, pl.ds(top - 2, 2)], 5, after)
+    faces_up = remote(face_x.at[:, pl.ds(top, 1)], face_x.at[:, pl.ds(end, 1)], 6, before)
+    early = [(wet_copy, has_before, has_after), (faces_down, has_after, has_before), (faces_up, has_before, has_after)]
+    rows_one, rows_two = 7, 7 + 2 * chunks
+    for copy, sends, _ in edges_one + early:
         guarded(sends, copy.start)
     send_rows(first, rows_one)
 
@@ -301,7 +307,7 @@
         def _():
             ref[:, start : start + 2] = jnp.zeros((ref.shape[0], 2, LANES), F32)
 
-    for ref in (first, second):
+    for ref in (face_x, first, second):
         clear(jnp.logical_not(has_before), ref, top - 2)
         clear(jnp.logical_not(has_after), ref, end)
     clear(jnp.logical_not(has_after), wet_after, 0)
@@ -366,7 +372,7 @@
             packs = tuple(pack(k, [second[at(f, h, k), top:end] for h in span], packs[f]) for f in range(3))
         return packs
 
-    for f, packed in enumerate(by_groups(0, depth, 5, pack_second, (blank,) * 3)):
+    for f, packed in enumerate(by_groups(0, depth, depth, pack_second, (blank,) * 3)):
         seam_own[4 + f] = packed
     get_surface.wait()
     for copy, _, receives in rims:
@@ -393,16 +399,13 @@
         return functools.reduce(jnp.add, tiles)
 
     partial = [own_product(a, b) for a, b in ((0, 0), (0, 1), (0, 2), (0, 3), (0, 4), (2, 3), (3, 3), (3, 4))]
-    small_lane = lane_index(8)
-    width = LANES // 2
-    while len(partial) > 1:
-        half = len(partial) // 2
-        take_first = (small_lane & (2 * width - 1)) < width
-        partial = [
-            jnp.where(take_first, a + roll(a, -width), b + roll(b, width)) for a, b in zip(partial[:half], partial[half:])
-        ]
-        width //= 2
-    slots[0:1] = jnp.sum(partial[0], axis=0, keepdims=True)
+    place = lax.broadcasted_iota(jnp.int32, (8, LANES), 0)
+    stacked = jnp.zeros((8, LANES), F32)
+    for g, p in enumerate(partial):
+        stacked = jnp.where(place == g, jnp.sum(p, axis=0, keepdims=True), stacked)
+    stacked = jnp.broadcast_to(jnp.sum(stacked, axis=1, keepdims=True), (8, LANES))
+    mine = jnp.where((lane_index(8) >> 4) == place, stacked, 0.0)
+    slots[0:1] = jnp.sum(mine, axis=0, keepdims=True)
 
     def sum_copy(i, device):
         return pltpu.make_async_remote_copy(
@@ -423,7 +426,7 @@
         guarded(sends, copy.start)
     send_rows(second, rows_two)
 
-    for copy, sends, receives in edges_one + [(wet_copy, has_before, has_after)]:
+    for copy, sends, receives in edges_one:
         guarded(sends, copy.wait_send)
         guarded(receives, copy.wait_recv)
 
@@ -441,7 +444,7 @@
                     ends[f * depth + k] = roll(packed, LANES - 4 * k)
             return carry
 
-        by_groups(0, depth, 5, one_group, 0)
+        by_groups(0, depth, depth, one_group, 0)
 
     def both_sides(f):
         return jnp.where(inner_side, seam_left[f], seam_right[f])
@@ -456,13 +459,13 @@
                 open_y[i] = vy[i] * wet_at(h, k) * wets_ahead[h] * (1.0 / 12.0)
         return carry
 
-    by_groups(0, depth, 5, open_columns, 0)
+    by_groups(0, depth, depth, open_columns, 0)
     get_forcing.wait()
     for h in span:
         theta[h * depth] = theta[h * depth] + forcing[:, h * LANES : (h + 1) * LANES] * wet_at(h, 0)
 
-    def column_shifts(ref, f, k, beyond):
-        centre = [ref[at(f, h, k), top:end] for h in span]
+    def column_shifts(ref, where, f, k, beyond):
+        centre = [ref[where(f, h, k), top:end] for h in span]
         return {s: shifted(centre, ends[beyond * depth + k], s, lane) for s in (-2, -1, 1, 2)}
 
     def face_shifts(k, steps):
@@ -475,24 +478,49 @@
                 guarded(sends, copy.wait_send)
             guarded(receives, copy.wait_recv)
 
+    def arms(u, wets):
+        v = [wets * x for x in u]
+        back, here = 7.0 * v[1], 7.0 * v[2]
+        return v[0], back + v[0], back - here, here + v[3], v[3]
+
+    for copy, sends, receives in early:
+        guarded(sends, copy.wait_send)
+        guarded(receives, copy.wait_recv)
+
+    def coefficients(levels, carry):
+        for k in levels:
+            for h in span:
+                i = h * depth + k
+                face_x[i, top - 1 : top] = face_x[i, top - 1 : top] * wet[i, 0:1]
+                face_x[i, end - 1 : end] = face_x[i, end - 1 : end] * wet_after[i, 0:1]
+        moved = [face_shifts(k, (-2, -1, 1)) for k in levels]
+        for k, uy in zip(levels, moved):
+            for h in span:
+                i = h * depth + k
+                wets = wet_at(h, k)
+                r = arms([face_x[i, top + s : end + s] for s in (-2, -1, 0, 1)], wets)
+                c = arms([uy[-2][h], uy[-1][h], open_y[i], uy[1][h]], wets)
+                for n, w in enumerate([(1.0 + r[2]) + c[2], r[0], r[3], c[0], c[3], r[1], r[4], c[1], c[4]]):
+                    cross[9 * i + n] = w
+        return carry
+
+    by_groups(0, depth, GROUP, coefficients, 0)
+
     def forward_down(levels, carry):
         got_rows(first, rows_one, levels, True)
-        for k in levels:
-            for h in span:
-                f, i = at(2, h, k), h * depth + k
-                first[f, top - 1 : top] = first[f, top - 1 : top] * wet[i, 0:1]
-                first[f, end - 1 : end] = first[f, end - 1 : end] * wet_after[i, 0:1]
-        moved = [(face_shifts(k, (-1,)), [column_shifts(first, f, k, f) for f in range(2)]) for k in levels]
+        moved = [
+            (face_shifts(k, (-1,)), [column_shifts(first, at_first, f, k, f) for f in range(2)]) for k in levels
+        ]
         for k, (uy, turned) in zip(levels, moved):
             out = []
             for h in span:
                 i = h * depth + k
                 found = []
                 for f, raw in ((0, theta), (1, salt)):
-                    q = [first[at(f, h, k), top + s : end + s] for s in (-2, -1, 0, 1, 2)]
+                    q = [first[at_first(f, h, k), top + s : end + s] for s in (-2, -1, 0, 1, 2)]
                     c = turned[f]
-                    row_here = first[at(2, h, k), top:end] * (7.0 * (q[2] + q[3]) - (q[1] + q[4]))
-                    row_back = first[at(2, h, k), top - 1 : end - 1] * (7.0 * (q[1] + q[2]) - (q[0] + q[3]))
+                    row_here = face_x[i, top:end] * (7.0 * (q[2] + q[3]) - (q[1] + q[4]))
+                    row_back = face_x[i, top - 1 : end - 1] * (7.0 * (q[1] + q[2]) - (q[0] + q[3]))
                     col_here = open_y[i] * (7.0 * (q[2] + c[1][h]) - (c[-1][h] + c[2][h]))
                     col_back = uy[-1][h] * (7.0 * (c[-1][h] + q[2]) - (c[-2][h] + c[1][h]))
                     value = raw[i] - (row_here - row_back) - (col_here - col_back)
@@ -526,29 +554,8 @@
 
     by_groups(0, depth - 1, 4, forward_up, carry)
 
-    def arms(u, wets):
-        v = [wets * x for x in u]
-        back, here = 7.0 * v[1], 7.0 * v[2]
-        return v[0], back + v[0], back - here, here + v[3], v[3]
-
-    def coefficients(levels, carry):
-        moved = [face_shifts(k, (-2, -1, 1)) for k in levels]
-        for k, uy in zip(levels, moved):
-            for h in span:
-                i = h * depth + k
-                wets = wet_at(h, k)
-                r = arms([first[at(2, h, k), top + s : end + s] for s in (-2, -1, 0, 1)], wets)
-                c = arms([uy[-2][h], uy[-1][h], open_y[i], uy[1][h]], wets)
-                for n, w in enumerate([(1.0 + r[2]) + c[2], r[0], r[3], c[0], c[3], r[1], r[4], c[1], c[4]]):
-                    cross[9 * i + n] = w
-        return carry
-
-    by_groups(0, depth, GROUP, coefficients, 0)
-
     others(lambda i, device: sum_copy(i, device).wait_recv())
     total = jnp.broadcast_to(jnp.sum(slots[...], axis=0, keepdims=True), (8, LANES))
-    for step in (8, 4, 2, 1):
-        total = total + roll(total, -step)
     m = [jnp.broadcast_to(total[:, 16 * g : 16 * g + 1], (8, LANES)) for g in range(8)]
     m = m[:5] + [2.0 * m[5] - m[1], 2.0 * m[6] - m[0], 2.0 * m[7] - m[1]]
     weights = [jnp.concatenate([w] * (wide[0] // 8), axis=0) for w in weights_from(m)]
@@ -571,7 +578,7 @@
             ends[5 * depth + k] = turned[1] - 0.15 * lifted
         return carry
 
-    by_groups(0, depth, 5, unpack_mu, 0)
+    by_groups(0, depth, depth, unpack_mu, 0)
 
     def finish(levels, carry):
         got_rows(second, rows_two, levels, True)
@@ -581,7 +588,7 @@
                 lifted = second[at(2, h, k), area] * zeta[h + 1, area]
                 second[at(0, h, k), area] = second[at(0, h, k), area] + 0.2 * lifted
                 second[at(1, h, k), area] = second[at(1, h, k), area] - 0.15 * lifted
-        moved = [[column_shifts(second, f, k, 4 + f) for f in range(2)] for k in levels]
+        moved = [[column_shifts(second, at, f, k, 4 + f) for f in range(2)] for k in levels]
         for k, turned in zip(levels, moved):
             for h in span:
                 i = h * depth + k
@@ -615,7 +622,13 @@
 def write_kernel(*refs):
     count = (len(refs) - 1) // 2
     sems = refs[-1]
-    copies = [pltpu.make_async_copy(refs[i], refs[count + i], sems.at[i]) for i in range(count)]
+    copies = []
+    for i in range(count):
+        pieces = 1
+        bounds = [refs[i].shape[0] * n // pieces for n in range(pieces + 1)]
+        for first, last in zip(bounds, bounds[1:]):
+            part = pl.ds(first, last - first)
+            copies.append(pltpu.make_async_copy(refs[i].at[part], refs[count + i].at[part], sems.at[len(copies)]))
     for copy in copies:
         copy.start()
     for copy in copies:
@@ -634,12 +647,13 @@
     ints = V((halves * depth, rows, LANES), jnp.int32)
     upper = V((halves * (depth - 1), rows, LANES), F32)
     tile = V((7, rows, LANES), F32)
-    halo = DMA((5 + 4 * (depth // GROUP),))
+    halo = DMA((7 + 4 * (depth // GROUP),))
     scratch = [
         flat, flat, flat, flat, ints, upper, V((rows, cols), F32), flat, flat,
         V((tall, cols + 2 * LANES), F32), V((tall, cols + 2 * LANES), jnp.int32),
         V((halves * depth, rows + RIM, LANES), F32), V((halves * depth, RIM, LANES), F32),
-        V((3 * halves * depth, tall, LANES), F32), V((3 * halves * depth, tall, LANES), F32),
+        V((halves * depth, tall, LANES), F32), V((2 * halves * depth, tall, LANES), F32),
+        V((3 * halves * depth, tall, LANES), F32),
         flat, flat, flat, flat, flat, flat,
         tile, tile, tile, V((7 * depth, rows, LANES), F32), V((count, LANES), F32),
         V((9 * halves * depth, rows, LANES), F32), upper, upper, V((ITERS * (halves + 2), tall, LANES), F32),
@@ -663,7 +677,7 @@
             out_shape=shapes,
             in_specs=[pl.BlockSpec(memory_space=V)] * len(outs),
             out_specs=[pl.BlockSpec(memory_space=pltpu.HBM)] * len(outs),
-            scratch_shapes=[DMA((len(outs),))],
+            scratch_shapes=[DMA((4 * len(outs),))],
             compiler_params=pltpu.CompilerParams(vmem_limit_bytes=1024 * 1024),
         )(*found)
     )

time: 20.2 us -> 19.6 us (0.970)
  Pallas kernels: 19.4 us -> 18.8 us
    pallas_call x1, Pallas kernels: 18.4 us -> 17.6 us  [shards(): pl.pallas_call(functools.partial(solve_kernel, (depth, rows, cols)), out_...]
where the time goes in v6:
time: 19.6 us; the launch traced here: 19.4 us
  Pallas kernels  18.8 us (96%)
  between operations  0.64 us (3%)
    pallas_call x1, Pallas kernels, shards(): pl.pallas_call(functools.partial(solve_kernel, (depth, rows, cols)), out_...  17.6 us
    pallas_call x1, Pallas kernels, shards(): pl.pallas_call(write_kernel, out_shape=shapes, in_specs=[pl.BlockSpec(mem...  1.16 us

profile of v6, /device:TPU:0, one launch (start us, length us, event | category | flops | bytes accessed | tf_op | source)
XLA Modules:
  0.0 19.4 jit_solution(14790279778020685054)
XLA Ops:
  0.6 17.6 %shard_map.138 = (f32[25,16,256]{2,1,0:T(8,128)S(1)}, f32[25,16,256]{2,1,0:T(8,128)S(1)}, f32[24,16,256]{2,1,0:T(8,128)S(1)}, f32[16,256]{1,0:T(8,128)S(1)}) custom-call(f32[25,16,256]{2,1,0:T(8,128)} %theta_in.1, f32[25,16,256]{2,1,0:T(8,128)} %salt_in.1, f32[25,16,256]{2,1,0:T(8,128)} %vx_in.1, f32[25,16,256]{2,1,0:T(8,128)} %vy_in.1, ...), custom_call_target="tpu_custom_call" | custom-call | tf_op jit(solution)/shard_map/pallas_call | solution.py:664
  18.3 1.2 %shard_map.139 = (f32[25,16,256]{2,1,0:T(8,128)}, f32[25,16,256]{2,1,0:T(8,128)}, f32[24,16,256]{2,1,0:T(8,128)}, f32[16,256]{1,0:T(8,128)}) custom-call(f32[25,16,256]{2,1,0:T(8,128)S(1)} %get-tuple-element.8.refs_0_, f32[25,16,256]{2,1,0:T(8,128)S(1)} %get-tuple-element.9.refs_1_, f32[24,16,256]{2,1,0:T(8,128)S(1)} %get-tuple-element.10.refs_2_, ...), custom_call_target="tpu_custom_call" | custom-call | tf_op jit(solution)/shard_map/pallas_call | solution.py:675

commit v7 on v6

--- a/solution.py
+++ b/solution.py
@@ -119,10 +119,10 @@
 def solve_kernel(
     sizes,
     theta_in, salt_in, vx_in, vy_in, land_in, kappa_in, forcing_in, bottom_in, theta_cot_in, salt_cot_in, surface_in,
-    theta_grad, salt_grad, kappa_grad, forcing_grad,
+    theta_grad, salt_grad, kappa_grad, forcing_grad, second, cross, zeta, ends,
     theta, salt, vx, vy, land, kappa, forcing, theta_cot, salt_cot,
-    surface, bottom, wet, wet_after, face_x, first, second, open_y, inverse, link, ratio, theta_mix, salt_mix,
-    seam_own, seam_left, seam_right, ends, slots, cross, k_fixed, k_zeta, zeta,
+    surface, bottom, wet, wet_after, face_x, first, open_y, inverse, link, ratio, theta_mix, salt_mix,
+    seam_own, seam_left, seam_right, slots, k_fixed, k_zeta,
     local_sem, rim_send, rim_recv, halo_send, halo_recv, sum_send, sum_recv,
 ):
     depth, rows, cols = sizes
@@ -473,7 +473,7 @@
         return {s: shifted(centre, ends[2 * depth + k], s, lane) for s in steps}
 
     def got_rows(ref, base, levels, sent_too):
-        for copy, sends, receives in row_copies(ref, base, lax.div(levels[0], GROUP)):
+        for copy, sends, receives in row_copies(ref, base, levels[0] // GROUP if isinstance(levels[0], int) else lax.div(levels[0], GROUP)):
             if sent_too:
                 guarded(sends, copy.wait_send)
             guarded(receives, copy.wait_recv)
@@ -504,10 +504,9 @@
                     cross[9 * i + n] = w
         return carry
 
-    by_groups(0, depth, GROUP, coefficients, 0)
+    by_groups(0, depth, depth, coefficients, 0)
 
     def forward_down(levels, carry):
-        got_rows(first, rows_one, levels, True)
         moved = [
             (face_shifts(k, (-1,)), [column_shifts(first, at_first, f, k, f) for f in range(2)]) for k in levels
         ]
@@ -531,7 +530,9 @@
             carry = tuple(out)
         return carry
 
-    carry = by_groups(0, depth, GROUP, forward_down, ((blank, blank),) * halves)
+    for g in range(chunks):
+        got_rows(first, rows_one, [g * GROUP], True)
+    carry = by_groups(0, depth, 25, forward_down, ((blank, blank),) * halves)
 
     def forward_up(steps, carry):
         for n in steps:
@@ -601,7 +602,7 @@
                     out[k, :, where] = signed_sum([cross[9 * i + n] * v for n, v in enumerate(values)])
         return carry
 
-    by_groups(0, depth, GROUP, finish, 0)
+    by_groups(0, theta_grad.shape[0], GROUP, finish, 0)
 
     def finish_kappa(levels, carry):
         for k in levels:
@@ -614,23 +615,69 @@
     for h in span:
         forcing_grad[:, h * LANES : (h + 1) * LANES] = zeta[h + 1, top:end] + wet_at(h, 0) * second[at(0, h, 0), top:end]
 
+    for g in range(theta_grad.shape[0] // GROUP, chunks):
+        got_rows(second, rows_two, [g * GROUP], True)
     for copy, sends, _ in rims:
         guarded(sends, copy.wait_send)
     others(lambda i, device: sum_copy(i, device).wait_send())
 
 
-def write_kernel(*refs):
-    count = (len(refs) - 1) // 2
-    sems = refs[-1]
+def finish_kernel(
+    sizes,
+    theta_done, salt_done, kappa_done, forcing_done, second, cross, zeta, ends,
+    theta_out, salt_out, kappa_out, forcing_out,
+    mu, theta_grad, salt_grad, sems,
+):
+    depth, rows, cols = sizes
+    halves = cols // LANES
+    top, end = RIM, RIM + rows
+    span = range(halves)
+    lane = lane_index(rows)
+    area = pl.ds(top - 2, rows + 8)
+    split = theta_done.shape[0]
     copies = []
-    for i in range(count):
-        pieces = 1
-        bounds = [refs[i].shape[0] * n // pieces for n in range(pieces + 1)]
-        for first, last in zip(bounds, bounds[1:]):
-            part = pl.ds(first, last - first)
-            copies.append(pltpu.make_async_copy(refs[i].at[part], refs[count + i].at[part], sems.at[len(copies)]))
-    for copy in copies:
+
+    def put(src, dst):
+        copy = pltpu.make_async_copy(src, dst, sems.at[len(copies)])
         copy.start()
+        copies.append(copy)
+
+    put(theta_done, theta_out.at[pl.ds(0, split)])
+    put(salt_done, salt_out.at[pl.ds(0, split)])
+    put(kappa_done, kappa_out)
+    put(forcing_done, forcing_out)
+
+    def at(f, h, k):
+        return (k * 3 + f) * halves + h
+
+    def mu_at(f, h, k):
+        return ((k - split) * 2 + f) * halves + h
+
+    def column_shifts(f, k):
+        centre = [mu[mu_at(f, h, k), top:end] for h in span]
+        return {s: shifted(centre, ends[(4 + f) * depth + k], s, lane) for s in (-2, -1, 1, 2)}
+
+    for first in range(split, depth, GROUP):
+        levels = range(first, min(depth, first + GROUP))
+        for k in levels:
+            for h in span:
+                lifted = second[at(2, h, k), area] * zeta[h + 1, area]
+                mu[mu_at(0, h, k), area] = second[at(0, h, k), area] + 0.2 * lifted
+                mu[mu_at(1, h, k), area] = second[at(1, h, k), area] - 0.15 * lifted
+        moved = [[column_shifts(f, k) for f in range(2)] for k in levels]
+        for k, turned in zip(levels, moved):
+            for h in span:
+                i = h * depth + k
+                where = slice(h * LANES, (h + 1) * LANES)
+                for f, out in ((0, theta_grad), (1, salt_grad)):
+                    values = [mu[mu_at(f, h, k), top + s : end + s] for s in (0, -2, 1)]
+                    values += [turned[f][s][h] for s in (-2, 1)]
+                    values += [mu[mu_at(f, h, k), top + s : end + s] for s in (-1, 2)]
+                    values += [turned[f][s][h] for s in (-1, 2)]
+                    out[k - split, :, where] = signed_sum([cross[9 * i + n] * v for n, v in enumerate(values)])
+        here, there = pl.ds(first - split, len(levels)), pl.ds(first, len(levels))
+        put(theta_grad.at[here], theta_out.at[there])
+        put(salt_grad.at[here], salt_out.at[there])
     for copy in copies:
         copy.wait()
 
@@ -653,32 +700,36 @@
         V((tall, cols + 2 * LANES), F32), V((tall, cols + 2 * LANES), jnp.int32),
         V((halves * depth, rows + RIM, LANES), F32), V((halves * depth, RIM, LANES), F32),
         V((halves * depth, tall, LANES), F32), V((2 * halves * depth, tall, LANES), F32),
-        V((3 * halves * depth, tall, LANES), F32),
         flat, flat, flat, flat, flat, flat,
-        tile, tile, tile, V((7 * depth, rows, LANES), F32), V((count, LANES), F32),
-        V((9 * halves * depth, rows, LANES), F32), upper, upper, V((ITERS * (halves + 2), tall, LANES), F32),
+        tile, tile, tile, V((count, LANES), F32), upper, upper,
         DMA((3 + 8 * halves,)), DMA((16,)), DMA((16,)), halo, halo, DMA((count,)), DMA((count,)),
     ]
     outs = [(depth, rows, cols), (depth, rows, cols), (depth - 1, rows, cols), (rows, cols)]
-    shapes = [jax.ShapeDtypeStruct(o, F32) for o in outs]
+    split = depth // GROUP * 3 // 5 * GROUP
+    parts = [
+        (split, rows, cols), (split, rows, cols), outs[2], outs[3], (3 * halves * depth, tall, LANES),
+        (9 * halves * depth, rows, LANES), (ITERS * (halves + 2), tall, LANES), (7 * depth, rows, LANES),
+    ]
     found = pl.pallas_call(
         functools.partial(solve_kernel, (depth, rows, cols)),
-        out_shape=shapes,
+        out_shape=[jax.ShapeDtypeStruct(o, F32) for o in parts],
         in_specs=[pl.BlockSpec(memory_space=pltpu.HBM)] * len(args),
-        out_specs=[pl.BlockSpec(memory_space=V)] * len(outs),
+        out_specs=[pl.BlockSpec(memory_space=V)] * len(parts),
         scratch_shapes=scratch,
         compiler_params=pltpu.CompilerParams(
-            collective_id=0, has_side_effects=True, vmem_limit_bytes=40 * 1024 * 1024
+            collective_id=0, has_side_effects=True, vmem_limit_bytes=32 * 1024 * 1024
         ),
     )(*[pltpu.with_memory_space_constraint(a, pltpu.HBM) for a in args])
+    left = (depth - split, rows, cols)
     return tuple(
         pl.pallas_call(
-            write_kernel,
-            out_shape=shapes,
-            in_specs=[pl.BlockSpec(memory_space=V)] * len(outs),
+            functools.partial(finish_kernel, (depth, rows, cols)),
+            out_shape=[jax.ShapeDtypeStruct(o, F32) for o in outs],
+            in_specs=[pl.BlockSpec(memory_space=V)] * len(parts),
             out_specs=[pl.BlockSpec(memory_space=pltpu.HBM)] * len(outs),
-            scratch_shapes=[DMA((4 * len(outs),))],
-            compiler_params=pltpu.CompilerParams(vmem_limit_bytes=1024 * 1024),
+            scratch_shapes=[V((2 * halves * left[0], tall, LANES), F32), V(left, F32), V(left, F32)]
+            + [DMA((4 + 2 * (left[0] // GROUP + 1),))],
+            compiler_params=pltpu.CompilerParams(vmem_limit_bytes=8 * 1024 * 1024),
         )(*found)
     )
 

time: 19.6 us -> 19.2 us (0.980)
  Pallas kernels: 18.8 us -> 18.3 us
    pallas_call x1, Pallas kernels: 17.6 us -> 17.1 us  [shards(): pl.pallas_call(functools.partial(solve_kernel, (depth, rows, cols)), out_...]
where the time goes in v7:
time: 19.2 us; the launch traced here: 18.9 us
  Pallas kernels  18.3 us (95%)
  between operations  0.64 us (3%)
    pallas_call x1, Pallas kernels, shards(): pl.pallas_call(functools.partial(solve_kernel, (depth, rows, cols)), out_...  17.1 us
    pallas_call x1, Pallas kernels, shards(): pl.pallas_call(functools.partial(finish_kernel, (depth, rows, cols)), out...  1.15 us

profile of v7, /device:TPU:0, one launch (start us, length us, event | category | flops | bytes accessed | tf_op | source)
XLA Modules:
  0.0 18.9 jit_solution(13377355916670344719)
XLA Ops:
  0.6 17.1 %shard_map.138 = (f32[15,16,256]{2,1,0:T(8,128)S(1)}, f32[15,16,256]{2,1,0:T(8,128)S(1)}, f32[24,16,256]{2,1,0:T(8,128)S(1)}, f32[16,256]{1,0:T(8,128)S(1)}, f32...) custom-call(f32[25,16,256]{2,1,0:T(8,128)} %theta_in.1, ...), custom_call_target="tpu_custom_call" | custom-call | tf_op jit(solution)/shard_map/pallas_call | solution.py:713
  17.8 1.2 %shard_map.139 = (f32[25,16,256]{2,1,0:T(8,128)}, f32[25,16,256]{2,1,0:T(8,128)}, f32[24,16,256]{2,1,0:T(8,128)}, f32[16,256]{1,0:T(8,128)}) custom-call(f32[15,16,256]{2,1,0:T(8,128)S(1)} %get-tuple-element.12.theta_done, f32[15,16,256]{2,1,0:T(8,128)S(1)} %get-tuple-element.13.salt_done, f32[24,16,256]{2,1,0:T(8,128)S(1)} %get-tuple-element.14.kappa_done, ...), custom_call_target="tpu_custom_call" | custom-call | tf_op jit(solution)/shard_map/pallas_call | solution.py:725

commit v8 on v7

--- a/solution.py
+++ b/solution.py
@@ -165,7 +165,14 @@
 
         lax.fori_loop(1, mesh_rows, one_row, 0)
 
-    others(lambda i, device: pl.semaphore_signal(barrier, inc=1, device_id=device, device_id_type=MESH))
+    def farthest_first(action):
+        for dr in sorted(range(mesh_rows), key=lambda d: abs(2 * d - mesh_rows)):
+            there = lax.rem(row + dr, mesh_rows)
+            for dc in sorted(range(mesh_cols), key=lambda d: abs(2 * d - mesh_cols)):
+                if dr or dc:
+                    action(dr * mesh_cols + dc, (there, lax.rem(col + dc, mesh_cols)))
+
+    farthest_first(lambda i, device: pl.semaphore_signal(barrier, inc=1, device_id=device, device_id_type=MESH))
 
     started = []
 
@@ -417,7 +424,7 @@
             device_id_type=MESH,
         )
 
-    others(lambda i, device: sum_copy(i, device).start())
+    farthest_first(lambda i, device: sum_copy(i, device).start())
     for k in range(ITERS):
         for h in range(halves + 2):
             zeta[k * (halves + 2) + h] = basis[k][:, h * LANES : (h + 1) * LANES]

time: 19.2 us -> 19.2 us (level)
  no operation moved by 1% of the time
where the time goes in v8:
time: 19.2 us; the launch traced here: 19 us
  Pallas kernels  18.4 us (96%)
  between operations  0.64 us (3%)
    pallas_call x1, Pallas kernels, shards(): pl.pallas_call(functools.partial(solve_kernel, (depth, rows, cols)), out_...  17.2 us
    pallas_call x1, Pallas kernels, shards(): pl.pallas_call(functools.partial(finish_kernel, (depth, rows, cols)), out...  1.15 us

profile of v8, /device:TPU:0, one launch (start us, length us, event | category | flops | bytes accessed | tf_op | source)
XLA Modules:
  0.0 19.0 jit_solution(4359245103597878496)
XLA Ops:
  0.6 17.2 %shard_map.138 = (f32[15,16,256]{2,1,0:T(8,128)S(1)}, f32[15,16,256]{2,1,0:T(8,128)S(1)}, f32[24,16,256]{2,1,0:T(8,128)S(1)}, f32[16,256]{1,0:T(8,128)S(1)}, f32...) custom-call(f32[25,16,256]{2,1,0:T(8,128)} %theta_in.1, ...), custom_call_target="tpu_custom_call" | custom-call | tf_op jit(solution)/shard_map/pallas_call | solution.py:720
  17.9 1.2 %shard_map.139 = (f32[25,16,256]{2,1,0:T(8,128)}, f32[25,16,256]{2,1,0:T(8,128)}, f32[24,16,256]{2,1,0:T(8,128)}, f32[16,256]{1,0:T(8,128)}) custom-call(f32[15,16,256]{2,1,0:T(8,128)S(1)} %get-tuple-element.12.theta_done, f32[15,16,256]{2,1,0:T(8,128)S(1)} %get-tuple-element.13.salt_done, f32[24,16,256]{2,1,0:T(8,128)S(1)} %get-tuple-element.14.kappa_done, ...), custom_call_target="tpu_custom_call" | custom-call | tf_op jit(solution)/shard_map/pallas_call | solution.py:732
